TPU v7x, 256 devices: a whole 4x4x8 slice. The times are simulated.
256 devices in a mesh: sec: 4 (over x_hi, core), dom: 64 (over y, z, x_lo).
Axes of the slice: x: 4 (x_hi: 2, x_lo: 2; x = x_hi * 2 + x_lo), y: 4, z: 8, core: 2. Of those that a mesh axis runs over, the one named last changes fastest.
Arguments:
- actuator_fields: float32 [16, 512, 4096], P(None, 'dom', 'sec'), may hold values from -6 to 6
- sensor_fields: float32 [8, 512, 4096], P(None, 'dom', 'sec'), may hold values from -6 to 6
- region_ids: int32 [512, 4096], P('dom', 'sec'), may hold values from 0 to 15
- stiffness_table: float32 [16], replicated, may hold values from 1 to 4
- density_table: float32 [16], replicated, may hold values from 1 to 2
- supported: int32 [10, 64, 32], P(None, 'dom', 'sec'), may hold values 0 or 1
Outputs:
- final_position: float32 [24, 512, 4096], P(None, 'dom', 'sec')
- cross: float32 [160, 80], P('sec')
All inputs are finite; a program needn't handle non-finite values. No bound on the sum of `supported` on one device may be relied on, other than what follows from the above.
Results may differ from a plain program's by a relative error of at most 0.0028.
Values sent between devices are 32-bit elements; how exact they have to be, the bound alone decides.
No kernel may reach another device: no remote copies, remote signals or barrier semaphores. Data moves between devices by JAX's collectives and lax.ppermute only.
A program may use at most 64 MiB of HBM per device.

v0:
```python
import math

import jax
import jax.numpy as jnp
from jax import lax
from jax.experimental import pallas as pl
from jax.experimental.pallas import tpu as pltpu
from jax.sharding import PartitionSpec as P


ROWS = 8
COLS = 1024
HALF = 512
LANES = 128
TILES = 5
WIDE = TILES * LANES
HALO = 20
ACT = 16
SENS = 8
RESP = ACT + SENS
SETS = RESP // 8
SNAPS = 10
STEPS = 20
REGIONS = 16
SLABS = ROWS * SETS + 1
NEAR = 3
FAR = NEAR * SETS + 1
OWN = 24
SHARE = 40
CELLS = 512 * 4096
FLAG_LANE = 112
UNROLL = 4
ALL_ROWS = 64
DT = 0.35


def block_column(shape, dim):
    spot = lax.broadcasted_iota(jnp.int32, shape, dim)
    return (spot & (LANES - 1)) * TILES + (spot >> 7)


MATMUL = (((1,), (0,)), ((), ()))
FAST = dict(preferred_element_type=jnp.float32)
EXACT = dict(precision=lax.Precision.HIGHEST, preferred_element_type=jnp.float32)


def one_hot(hit):
    return jnp.where(hit, 1.0, 0.0).astype(jnp.bfloat16)


def halves(cells):
    high = cells.astype(jnp.bfloat16)
    return high, (cells - high.astype(jnp.float32)).astype(jnp.bfloat16)


def pick_columns(parts, pick):
    return sum(lax.dot_general(part, pick, MATMUL, **FAST) for part in parts)


def turn_rows(parts, turn):
    return [lax.dot_general(turn, part, MATMUL, **FAST).astype(jnp.bfloat16) for part in parts]


def row_major(inverse=False):
    shape = (ROWS * RESP, ROWS * RESP)
    old = lax.broadcasted_iota(jnp.int32, shape, 0 if inverse else 1)
    new = lax.broadcasted_iota(jnp.int32, shape, 1 if inverse else 0)
    return one_hot(new == (old & (ROWS - 1)) * RESP + (old >> 3))


def edge_kernel(*refs):
    for act_ref, sens_ref, ids_ref, out_ref in (refs[0:3] + refs[6:7], refs[3:6] + refs[7:8]):
        out_ref[0:ACT] = act_ref[...]
        out_ref[ACT:RESP] = sens_ref[...]
        out_ref[RESP] = ids_ref[...].astype(jnp.float32) + 1.0


def edges(actuator_fields, sensor_fields, region_ids):
    def blocks(column):
        return [
            pl.BlockSpec((ACT, ROWS, LANES), lambda i, c=column: (0, 0, c)),
            pl.BlockSpec((SENS, ROWS, LANES), lambda i, c=column: (0, 0, c)),
            pl.BlockSpec((ROWS, LANES), lambda i, c=column: (0, c)),
        ]

    out = jax.ShapeDtypeStruct((RESP + 1, ROWS, LANES), jnp.float32)
    whole = pl.BlockSpec((RESP + 1, ROWS, LANES), lambda i: (0, 0, 0))
    fields = (actuator_fields, sensor_fields, region_ids)
    return pl.pallas_call(
        edge_kernel,
        grid=(1,),
        out_shape=(out, out),
        in_specs=blocks(COLS // LANES - 1) + blocks(0),
        out_specs=(whole, whole),
    )(*fields, *fields)


def main_kernel(act_ref, sens_ref, ids_ref, sup_ref, first_ref, second_ref):
    turn = row_major()
    cells = jnp.concatenate(
        [act_ref[...].reshape(ACT * ROWS, COLS), sens_ref[...].reshape(SENS * ROWS, COLS)], axis=0
    )
    parts = turn_rows(halves(cells), turn)
    ids = (ids_ref[...].astype(jnp.float32) + 1.0).astype(jnp.bfloat16)
    shape = (WIDE, WIDE)
    column = block_column(shape, 1)
    source = lax.broadcasted_iota(jnp.int32, shape, 0)
    inner = column < HALF + HALO
    outer = column >= WIDE - HALO
    for out_ref, begin, wanted in (
        (first_ref, 0, jnp.where(inner, column, -1)),
        (second_ref, COLS - WIDE, jnp.where(column < HALF, column + LANES, jnp.where(outer, column - HALF, -1))),
    ):
        pick = one_hot(source == wanted)
        cut = slice(begin, begin + WIDE)
        out_ref[0 : SLABS - 1] = pick_columns([part[:, cut] for part in parts], pick).reshape(SLABS - 1, 8, WIDE)
        out_ref[SLABS - 1] = pick_columns([ids[:, cut]], pick)
        out_ref[SLABS - 1, :, FLAG_LANE : FLAG_LANE + SNAPS] = sup_ref[...].astype(jnp.float32)


def halo_kernel(side_ref, first_ref, second_ref, left_ref, right_ref, keep_ref, give_ref, far_keep_ref, far_give_ref):
    turn = row_major()
    shape = (LANES, WIDE)
    column = block_column(shape, 1)
    source = lax.broadcasted_iota(jnp.int32, shape, 0)
    blocks = []
    for in_ref, edge_ref, hit in (
        (first_ref, left_ref, (column >= WIDE - HALO) & (source == column - HALF)),
        (second_ref, right_ref, (column >= HALF) & (column < HALF + HALO) & (source == column - HALF)),
    ):
        pick = one_hot(hit)
        parts = turn_rows(halves(edge_ref[0:RESP].reshape(RESP * ROWS, LANES)), turn)
        fields = in_ref[0 : SLABS - 1] + pick_columns(parts, pick).reshape(SLABS - 1, 8, WIDE)
        ids = in_ref[SLABS - 1] + pick_columns([edge_ref[RESP].astype(jnp.bfloat16)], pick)
        blocks.append((fields, ids))
    low_side = side_ref[0] == 0
    (fields_0, ids_0), (fields_1, ids_1) = blocks
    near = NEAR * SETS
    for out_ref, far_ref, fields, ids in (
        (keep_ref, far_keep_ref, jnp.where(low_side, fields_0, fields_1), jnp.where(low_side, ids_0, ids_1)),
        (give_ref, far_give_ref, jnp.where(low_side, fields_1, fields_0), jnp.where(low_side, ids_1, ids_0)),
    ):
        out_ref[0 : SLABS - 1] = fields
        out_ref[SLABS - 1] = ids
        far_ref[0:near] = jnp.where(low_side, fields[:near], fields[SLABS - 1 - near :])
        far_ref[near] = ids


def after(cells):
    return jnp.concatenate([cells[:, LANES:], pltpu.roll(cells[:, :LANES], LANES - 1, 1)], axis=1)


def wave_kernel(
    side_ref, place_ref, stiff_ref, dens_ref,
    keep_ref, give_ref, keep_up_ref, give_up_ref, keep_dn_ref, give_dn_ref, far_keep_ref, far_give_ref,
    own_ref, other_ref, piece_0_ref, piece_1_ref, piece_2_ref, piece_3_ref,
    p_ref, u_ref, s_ref, m_ref, fx_ref, fy_ref, fw_ref, mk_ref, mask_ref, fa_ref, fs_ref, acc_ref,
):
    side = side_ref[0]
    own_base = 8 * side
    other_base = 8 - own_base
    strips = (
        (keep_ref, OWN + own_base), (give_ref, OWN + other_base),
        (keep_up_ref, OWN - 16 + own_base), (give_up_ref, OWN - 16 + other_base),
        (keep_dn_ref, OWN + 16 + own_base), (give_dn_ref, OWN + 16 + other_base),
    )

    def materials(ids, base):
        stiff = jnp.zeros_like(ids)
        dens = jnp.zeros_like(ids)
        for region in range(REGIONS):
            here = ids == region + 1.0
            stiff = jnp.where(here, stiff_ref[region], stiff)
            dens = jnp.where(here, dens_ref[region], dens)
        inside = ids > 0.0
        rows = pl.ds(pl.multiple_of(base, 8), 8)
        s_ref[rows, :] = stiff
        m_ref[rows, :] = jnp.where(inside, (0.5 * DT * DT) / jnp.where(inside, dens, 1.0), 0.0)

    for ref, base in strips:
        materials(ref[SLABS - 1], base)
    shape = (8, WIDE)
    tile = 4 * side + (block_column(shape, 1) >> 7)
    inside = block_column(shape, 1) < HALF
    spread = one_hot(inside & (lax.broadcasted_iota(jnp.int32, shape, 0) == tile))
    for ref, strip in ((keep_ref, side), (give_ref, 1 - side)):
        flags = ref[SLABS - 1, :, 0:LANES].astype(jnp.bfloat16)
        masks = lax.dot_general(flags, spread, (((0,), (0,)), ((), ())), **FAST)
        mask_ref[strip] = masks[FLAG_LANE:LANES]
    last_strip = ALL_ROWS - 8
    far = ((far_keep_ref, side), (far_give_ref, 1 - side))
    for ref, above in far:
        materials(ref[FAR - 1], last_strip * (1 - above))

    def coefficients(turn, carry):
        for extra in range(9):
            row = 1 + turn * 9 + extra
            centre = jnp.broadcast_to(s_ref[pl.ds(row, 1), :], (8, WIDE))
            upper = jnp.broadcast_to(s_ref[pl.ds(row - 1, 1), :], (8, WIDE))
            fx_ref[row] = centre + upper
            fy_ref[row] = centre + after(centre)
            fw_ref[row] = centre[:, :LANES] + pltpu.roll(centre[:, WIDE - LANES :], 1, 1)
            mk_ref[row] = jnp.broadcast_to(m_ref[pl.ds(row, 1), :], (8, WIDE))
        return carry

    lax.fori_loop(0, (ALL_ROWS - 1) // 9, coefficients, 0)

    def place(slab, row, set_index):
        begin = slab * (mk_ref[row] * (DT / (0.5 * DT * DT)))
        u_ref[row * SETS + set_index] = begin
        p_ref[row * SETS + set_index] = begin

    for ref, base in strips:
        def fill(row, carry, ref=ref, base=base):
            for set_index in range(SETS):
                place(ref[row * SETS + set_index], base + row, set_index)
            return carry

        lax.fori_loop(0, ROWS, fill, 0)
    for ref, above in far:
        base = above * (8 - NEAR) + last_strip * (1 - above)
        for row in range(NEAR):
            for set_index in range(SETS):
                place(ref[row * SETS + set_index], base + row, set_index)

    def step(count):
        first = OWN - STEPS + 1 + count
        rows = 16 + 2 * (STEPS - 1) - 2 * count

        def start(set_index):
            centre = p_ref[first * SETS + set_index]
            north = fx_ref[first] * (centre - p_ref[(first - 1) * SETS + set_index])
            return centre, north

        def one(row, carry):
            face = fx_ref[row + 1]
            along = fy_ref[row]
            back = fw_ref[row]
            mass = mk_ref[row]
            done = []
            for set_index, (centre, north) in enumerate(carry):
                spot = row * SETS + set_index
                below = p_ref[spot + SETS]
                south = face * (below - centre)
                east = along * (after(centre) - centre)
                first_west = back * (centre[:, :LANES] - pltpu.roll(centre[:, WIDE - LANES :], 1, 1))
                west = jnp.concatenate([first_west, east[:, : WIDE - LANES]], axis=1)
                speed = u_ref[spot] + mass * ((south - north) + (east - west))
                u_ref[spot] = speed
                p_ref[spot] = centre + speed
                done.append((below, south))
            return tuple(done)

        def several(turn, carry):
            row = first + UNROLL * turn
            for extra in range(UNROLL):
                carry = one(row + extra, carry)
            return carry

        begin = tuple(start(set_index) for set_index in range(SETS))
        lax.fori_loop(0, (rows + UNROLL - 1) // UNROLL, several, begin)

    def snapshot(index):
        act_rows = pl.ds(pl.multiple_of(index * ACT, ACT), ACT)
        sens_rows = pl.ds(pl.multiple_of(index * SENS, SENS), SENS)
        for strip in range(2):
            mask = jnp.broadcast_to(mask_ref[strip, pl.ds(index, 1), :], (8, WIDE))
            fast = mask * (1.0 / DT)

            def keep_rows(turn, carry, strip=strip, mask=mask, fast=fast):
                for extra in range(4):
                    at = turn * 4 + extra + 8 * strip
                    spot = (OWN + at) * SETS
                    place_act = jnp.concatenate([p_ref[spot] * mask, p_ref[spot + 1] * mask], axis=0)
                    speed_act = jnp.concatenate([u_ref[spot] * fast, u_ref[spot + 1] * fast], axis=0)
                    fa_ref[at, act_rows, 0:WIDE] = place_act.astype(jnp.bfloat16)
                    fa_ref[at, act_rows, WIDE : 2 * WIDE] = speed_act.astype(jnp.bfloat16)
                    fs_ref[at, sens_rows, 0:WIDE] = p_ref[spot + 2] * mask
                    fs_ref[at, sens_rows, WIDE : 2 * WIDE] = u_ref[spot + 2] * fast
                return carry

            lax.fori_loop(0, 2, keep_rows, 0)

    step(1)
    snapshot(0)

    def advance(index, carry):
        step(2 * index)
        step(2 * index + 1)
        snapshot(index)
        return carry

    lax.fori_loop(1, SNAPS, advance, 0)

    def gram(turn, total):
        for extra in range(4):
            row = 4 * turn + extra
            total = total + lax.dot_general(
                fa_ref[row], fs_ref[row].astype(jnp.bfloat16), (((1,), (1,)), ((), ())), **FAST
            )
        return total

    acc_ref[...] = lax.fori_loop(0, 4, gram, jnp.zeros((ACT * SNAPS, SENS * SNAPS), jnp.float32))
    shape = (ACT * SNAPS, ACT * SNAPS)
    old = lax.broadcasted_iota(jnp.int32, shape, 1)
    new = lax.broadcasted_iota(jnp.int32, shape, 0)
    turn = jnp.where(new == (old & (ACT - 1)) * SNAPS + (old >> 4), 1.0, 0.0)
    shape = (SENS * SNAPS, SENS * SNAPS)
    old = lax.broadcasted_iota(jnp.int32, shape, 0)
    new = lax.broadcasted_iota(jnp.int32, shape, 1)
    turn_back = jnp.where(new == (old & (SENS - 1)) * SNAPS + (old >> 3), 1.0, 0.0)
    turned = lax.dot_general(turn, acc_ref[...], MATMUL, **EXACT)
    acc_ref[...] = lax.dot_general(turned, turn_back, MATMUL, **EXACT) * (1.0 / math.sqrt(CELLS))
    place = place_ref[0]
    for hop, out_ref in enumerate((piece_0_ref, piece_1_ref, piece_2_ref, piece_3_ref)):
        out_ref[...] = acc_ref[pl.ds(pl.multiple_of(((place + hop) & 3) * SHARE, 8), SHARE), :]

    shape = (WIDE, HALF)
    pick = one_hot(lax.broadcasted_iota(jnp.int32, shape, 1) == block_column(shape, 0))
    turn = row_major(inverse=True)
    for out_ref, base in ((own_ref, OWN + own_base), (other_ref, OWN + other_base)):
        cells = p_ref[pl.ds(base * SETS, ROWS * SETS)].reshape(ROWS * RESP, WIDE)
        out_ref[...] = pick_columns(turn_rows(halves(cells), turn), pick).reshape(RESP, ROWS, HALF)


def advance_block(*operands):
    vmem = pl.BlockSpec(memory_space=pltpu.VMEM)
    smem = pl.BlockSpec(memory_space=pltpu.SMEM)
    part = jax.ShapeDtypeStruct((RESP, ROWS, HALF), jnp.float32)
    return pl.pallas_call(
        wave_kernel,
        out_shape=(part, part) + (jax.ShapeDtypeStruct((SHARE, SENS * SNAPS), jnp.float32),) * 4,
        in_specs=[smem] * 4 + [vmem] * 8,
        out_specs=(vmem,) * 6,
        scratch_shapes=[
            pltpu.VMEM((ALL_ROWS * SETS, 8, WIDE), jnp.float32),
            pltpu.VMEM((ALL_ROWS * SETS, 8, WIDE), jnp.float32),
            pltpu.VMEM((ALL_ROWS, WIDE), jnp.float32),
            pltpu.VMEM((ALL_ROWS, WIDE), jnp.float32),
            pltpu.VMEM((ALL_ROWS, 8, WIDE), jnp.float32),
            pltpu.VMEM((ALL_ROWS, 8, WIDE), jnp.float32),
            pltpu.VMEM((ALL_ROWS, 8, LANES), jnp.float32),
            pltpu.VMEM((ALL_ROWS, 8, WIDE), jnp.float32),
            pltpu.VMEM((2, LANES - FLAG_LANE, WIDE), jnp.float32),
            pltpu.VMEM((16, ACT * SNAPS, 2 * WIDE), jnp.bfloat16),
            pltpu.VMEM((16, SENS * SNAPS, 2 * WIDE), jnp.float32),
            pltpu.VMEM((ACT * SNAPS, SENS * SNAPS), jnp.float32),
        ],
        compiler_params=grant(40),
    )(*operands)


def along_dom(cells, distance):
    count = lax.axis_size("dom")
    return lax.ppermute(cells, "dom", [(i, i + distance) for i in range(count) if 0 <= i + distance < count])


def outward(cells, distance):
    count = lax.axis_size("dom")
    pairs = [(i, i + distance if i % 2 else i - distance) for i in range(count)]
    return lax.ppermute(cells, "dom", [(i, j) for i, j in pairs if 0 <= j < count])


def grant(mebibytes):
    return pltpu.CompilerParams(vmem_limit_bytes=mebibytes << 20)


def swap(cells, bit):
    count = lax.axis_size("dom")
    return lax.ppermute(cells, "dom", [(i, i ^ bit) for i in range(count)])


def body(actuator_fields, sensor_fields, region_ids, stiffness_table, density_table, supported):
    side = lax.axis_index("dom") % 2
    side_word = side.astype(jnp.int32).reshape(1)
    place_word = lax.axis_index("sec").astype(jnp.int32).reshape(1)
    sections = lax.axis_size("sec")
    right_edge, left_edge = edges(actuator_fields, sensor_fields, region_ids)
    left = lax.ppermute(right_edge, "sec", [(i, i + 1) for i in range(sections - 1)])
    right = lax.ppermute(left_edge, "sec", [(i + 1, i) for i in range(sections - 1)])
    flags = jnp.transpose(supported, (1, 2, 0)).reshape(-1, SNAPS)

    vmem = pl.BlockSpec(memory_space=pltpu.VMEM)
    smem = pl.BlockSpec(memory_space=pltpu.SMEM)
    block = jax.ShapeDtypeStruct((SLABS, 8, WIDE), jnp.float32)
    first, second = pl.pallas_call(
        main_kernel, out_shape=(block, block), in_specs=[vmem] * 4, out_specs=(vmem, vmem), compiler_params=grant(16)
    )(actuator_fields, sensor_fields, region_ids, flags)
    far = jax.ShapeDtypeStruct((FAR, 8, WIDE), jnp.float32)
    keep, give, far_keep, far_give = pl.pallas_call(
        halo_kernel,
        out_shape=(block, block, far, far),
        in_specs=[smem] + [vmem] * 4,
        out_specs=(vmem,) * 4,
        compiler_params=grant(16),
    )(side_word, first, second, left, right)

    got = swap(give, 1)
    keep_up, keep_dn = along_dom(keep, 2), along_dom(keep, -2)
    far_keep = outward(far_keep, 4)
    far_give = outward(far_give, 3)
    give_up = along_dom(got, 2)
    give_dn = along_dom(got, -2)

    own, other, *pieces = advance_block(
        side_word, place_word, stiffness_table, density_table,
        keep, got, keep_up, give_up, keep_dn, give_dn, far_keep, far_give,
    )
    total = pieces[0]
    for hop in range(1, sections):
        total = total + lax.ppermute(pieces[hop], "sec", [(i, (i + hop) % sections) for i in range(sections)])
    other, total = lax.optimization_barrier((other, total))
    back = swap(other, 1)
    position = jnp.where(
        side == 0, jnp.concatenate([own, back], 2), jnp.concatenate([back, own], 2)
    )
    for bits in (4, 12, 16, 48):
        total = total + swap(total, bits)
    position, total = lax.optimization_barrier((position, total))
    total = total + sum(swap(total, bits) for bits in (1, 2, 3))
    return (position, total)


def solution(mesh):
    in_specs = (
        P(None, "dom", "sec"),
        P(None, "dom", "sec"),
        P("dom", "sec"),
        P(),
        P(),
        P(None, "dom", "sec"),
    )
    out_specs = (P(None, "dom", "sec"), P("sec", None))
    return jax.shard_map(body, mesh=mesh, in_specs=in_specs, out_specs=out_specs, check_vma=False)
```

profile of v0, /device:TPU:56, one launch (start us, length us, event | category | flops | bytes accessed | tf_op | source)
XLA Modules:
  0.0 135.4 jit_solution(16138512742287255010)
XLA Ops:
  0.7 1.6 %shard_map.78 = (f32[25,8,128]{2,1,0:T(8,128)}, f32[25,8,128]{2,1,0:T(8,128)}) custom-call(f32[16,8,1024]{2,1,0:T(8,128)} %refs_3_.1, f32[8,8,1024]{2,1,0:T(8,128)} %refs_4_.1, s32[8,1024]{1,0:T(8,128)} %refs_5_.1, f32[16,8,1024]{2,1,0:T(8,128)} %refs_3_.1, f32[8,8,1024]{2,1,0:T(8,128)} %refs_4_.1, s32[8,1024]{1,0:T(8,128)} %refs_5_.1), custom_call_target="tpu_custom_call" | custom-call | tf_op jit(solution)/shard_map/pallas_call | solution.py:89
  2.3 1.7 %collective-permute-start = (f32[25,8,128]{2,1,0:T(8,128)}, f32[25,8,128]{2,1,0:T(8,128)S(1)}, u32[]{:S(2)}, u32[]{:S(2)}) collective-permute-start(f32[25,8,128]{2,1,0:T(8,128)} %get-tuple-element.22), channel_id=1, source_target_pairs={{0,64},{64,128},{128,192},{1,65},{65,129},{129,193},{2,66},{66,130... | collective-permute-start | bytes 307208 | tf_op jit(solution)/shard_map/ppermute | solution.py:379
  7.6 2.7 %collective-permute-done.1.right_ref = f32[25,8,128]{2,1,0:T(8,128)S(1)} collective-permute-done((f32[25,8,128]{2,1,0:T(8,128)}, f32[25,8,128]{2,1,0:T(8,128)S(1)}, u32[]{:S(2)}, u32[]{:S(2)}) %collective-permute-start.1) | collective-permute-done | bytes 102432 | tf_op jit(solution)/shard_map/ppermute | solution.py:380
  11.7 3.8 %collective-permute-start.3 = (f32[25,8,640]{2,1,0:T(8,128)S(1)}, f32[25,8,640]{2,1,0:T(8,128)S(1)}, u32[]{:S(2)}, u32[]{:S(2)}) collective-permute-start(f32[25,8,640]{2,1,0:T(8,128)S(1)} %get-tuple-element.24.keep_ref), channel_id=1, source_target_pairs={{0,2},{1,3},{2,4},{3,5},{4,6},{5,7},{6,8},{7,9},{8,10},{9,11},{10,... | collective-permute-start | bytes 1536008 | tf_op jit(solution)/shard_map/ppermute | solution.py:355
  15.6 2.0 %collective-permute-start.5 = (f32[25,8,640]{2,1,0:T(8,128)S(1)}, f32[25,8,640]{2,1,0:T(8,128)S(1)}, u32[]{:S(2)}, u32[]{:S(2)}) collective-permute-start(f32[25,8,640]{2,1,0:T(8,128)S(1)} %get-tuple-element.24.keep_ref), channel_id=1, source_target_pairs={{2,0},{3,1},{4,2},{5,3},{6,4},{7,5},{8,6},{9,7},{10,8},{11,9},{12,... | collective-permute-start | bytes 1536008 | tf_op jit(solution)/shard_map/ppermute | solution.py:355
  17.6 3.6 %collective-permute-done.2.give_ref = f32[25,8,640]{2,1,0:T(8,128)S(1)} collective-permute-done((f32[25,8,640]{2,1,0:T(8,128)S(1)}, f32[25,8,640]{2,1,0:T(8,128)S(1)}, u32[]{:S(2)}, u32[]{:S(2)}) %collective-permute-start.2) | collective-permute-done | bytes 512032 | tf_op jit(solution)/shard_map/ppermute | solution.py:370
  21.2 3.8 %collective-permute-start.4 = (f32[25,8,640]{2,1,0:T(8,128)S(1)}, f32[25,8,640]{2,1,0:T(8,128)S(1)}, u32[]{:S(2)}, u32[]{:S(2)}) collective-permute-start(f32[25,8,640]{2,1,0:T(8,128)S(1)} %collective-permute-done.2.give_ref), channel_id=1, source_target_pairs={{0,2},{1,3},{2,4},{3,5},{4,6},{5,7},{6,8},{7,9},{8,10},{9,11},{10,... | collective-permute-start | bytes 1536008 | tf_op jit(solution)/shard_map/ppermute | solution.py:355
  25.0 2.0 %collective-permute-start.6 = (f32[25,8,640]{2,1,0:T(8,128)S(1)}, f32[25,8,640]{2,1,0:T(8,128)S(1)}, u32[]{:S(2)}, u32[]{:S(2)}) collective-permute-start(f32[25,8,640]{2,1,0:T(8,128)S(1)} %collective-permute-done.2.give_ref), channel_id=1, source_target_pairs={{2,0},{3,1},{4,2},{5,3},{6,4},{7,5},{8,6},{9,7},{10,8},{11,9},{12,... | collective-permute-start | bytes 1536008 | tf_op jit(solution)/shard_map/ppermute | solution.py:355
  27.0 7.5 %collective-permute-start.7 = (f32[10,8,640]{2,1,0:T(8,128)S(1)}, f32[10,8,640]{2,1,0:T(8,128)S(1)}, u32[]{:S(2)}, u32[]{:S(2)}) collective-permute-start(f32[10,8,640]{2,1,0:T(8,128)S(1)} %get-tuple-element.26), channel_id=1, source_target_pairs={{1,5},{3,7},{4,0},{5,9},{6,2},{7,11},{8,4},{9,13},{10,6},{11,15},{... | collective-permute-start | bytes 614408 | tf_op jit(solution)/shard_map/ppermute | solution.py:361
  34.5 13.7 %collective-permute-done.7.far_keep_ref = f32[10,8,640]{2,1,0:T(8,128)S(1)} collective-permute-done((f32[10,8,640]{2,1,0:T(8,128)S(1)}, f32[10,8,640]{2,1,0:T(8,128)S(1)}, u32[]{:S(2)}, u32[]{:S(2)}) %collective-permute-start.7) | collective-permute-done | bytes 204832 | tf_op jit(solution)/shard_map/ppermute | solution.py:361
  48.9 3.6 %collective-permute-start.8 = (f32[10,8,640]{2,1,0:T(8,128)S(1)}, f32[10,8,640]{2,1,0:T(8,128)S(1)}, u32[]{:S(2)}, u32[]{:S(2)}) collective-permute-start(f32[10,8,640]{2,1,0:T(8,128)S(1)} %get-tuple-element.27), channel_id=1, source_target_pairs={{1,4},{3,6},{4,1},{5,8},{6,3},{7,10},{8,5},{9,12},{10,7},{11,14},{... | collective-permute-start | bytes 614408 | tf_op jit(solution)/shard_map/ppermute | solution.py:361
  52.5 8.3 %collective-permute-done.8.far_give_ref = f32[10,8,640]{2,1,0:T(8,128)S(1)} collective-permute-done((f32[10,8,640]{2,1,0:T(8,128)S(1)}, f32[10,8,640]{2,1,0:T(8,128)S(1)}, u32[]{:S(2)}, u32[]{:S(2)}) %collective-permute-start.8) | collective-permute-done | bytes 204832 | tf_op jit(solution)/shard_map/ppermute | solution.py:361
  63.4 26.8 %shard_map.80 = (f32[24,8,512]{2,1,0:T(8,128)S(1)}, f32[24,8,512]{2,1,0:T(8,128)}, f32[40,80]{1,0:T(8,128)S(1)}, f32[40,80]{1,0:T(8,128)S(1)}, f32[40,80]{1,0:T(8,128)S(1)}, /*index=5*/f32[40,80]{1,0:T(8,128)S(1)}) custom-call(s32[1]{0:T(128)} %bitcast.side_ref, s32[1]{0:T(128)} %bitcast.1.place_ref, f32[16]{0:T(128)S(1)} %copy-done.8, f32[16]{0:T(128)S(1)} %copy-done.9, ...), custom_call_target="tpu_custom_call" | custom-call | tf_op jit(solution)/shard_map/pallas_call | solution.py:330
  90.2 4.4 %collective-permute-start.10 = (f32[40,80]{1,0:T(8,128)S(1)}, f32[40,80]{1,0:T(8,128)S(1)}, u32[]{:S(2)}, u32[]{:S(2)}) collective-permute-start(f32[40,80]{1,0:T(8,128)S(1)} %get-tuple-element.32), channel_id=1, source_target_pairs={{0,128},{64,192},{128,0},{192,64},{1,129},{65,193},{129,1},{193,65... | collective-permute-start | bytes 38408 | tf_op jit(solution)/shard_map/ppermute | solution.py:411
  94.6 4.6 %collective-permute-start.11 = (f32[40,80]{1,0:T(8,128)S(1)}, f32[40,80]{1,0:T(8,128)S(1)}, u32[]{:S(2)}, u32[]{:S(2)}) collective-permute-start(f32[40,80]{1,0:T(8,128)S(1)} %get-tuple-element.33), channel_id=1, source_target_pairs={{0,192},{64,0},{128,64},{192,128},{1,193},{65,1},{129,65},{193,129... | collective-permute-start | bytes 38408 | tf_op jit(solution)/shard_map/ppermute | solution.py:411
  100.7 3.2 %collective-permute-done.9 = f32[40,80]{1,0:T(8,128)S(1)} collective-permute-done((f32[40,80]{1,0:T(8,128)S(1)}, f32[40,80]{1,0:T(8,128)S(1)}, u32[]{:S(2)}, u32[]{:S(2)}) %collective-permute-start.9) | collective-permute-done | bytes 12832 | tf_op jit(solution)/shard_map/ppermute | solution.py:411
  104.8 3.9 %collective-permute-done.13 = f32[40,80]{1,0:T(8,128)S(1)} collective-permute-done((f32[40,80]{1,0:T(8,128)S(1)}, f32[40,80]{1,0:T(8,128)S(1)}, u32[]{:S(2)}, u32[]{:S(2)}) %collective-permute-start.13) | collective-permute-done | bytes 12832 | tf_op jit(solution)/shard_map/ppermute | solution.py:370
  110.1 4.6 %collective-permute-done.14 = f32[40,80]{1,0:T(8,128)S(1)} collective-permute-done((f32[40,80]{1,0:T(8,128)S(1)}, f32[40,80]{1,0:T(8,128)S(1)}, u32[]{:S(2)}, u32[]{:S(2)}) %collective-permute-start.14) | collective-permute-done | bytes 12832 | tf_op jit(solution)/shard_map/ppermute | solution.py:370
  115.4 3.1 %collective-permute-done.15 = f32[40,80]{1,0:T(8,128)S(1)} collective-permute-done((f32[40,80]{1,0:T(8,128)S(1)}, f32[40,80]{1,0:T(8,128)S(1)}, u32[]{:S(2)}, u32[]{:S(2)}) %collective-permute-start.15) | collective-permute-done | bytes 12832 | tf_op jit(solution)/shard_map/ppermute | solution.py:370
  118.5 5.0 %collective-permute-done.16 = f32[40,80]{1,0:T(8,128)S(1)} collective-permute-done((f32[40,80]{1,0:T(8,128)S(1)}, f32[40,80]{1,0:T(8,128)S(1)}, u32[]{:S(2)}, u32[]{:S(2)}) %collective-permute-start.16) | collective-permute-done | bytes 12832 | tf_op jit(solution)/shard_map/ppermute | solution.py:370
  124.4 1.9 %collective-permute-start.17 = (f32[40,80]{1,0:T(8,128)S(1)}, f32[40,80]{1,0:T(8,128)S(1)}, u32[]{:S(2)}, u32[]{:S(2)}) collective-permute-start(f32[40,80]{1,0:T(8,128)S(1)} %add.41), channel_id=1, source_target_pairs={{0,1},{1,0},{2,3},{3,2},{4,5},{5,4},{6,7},{7,6},{8,9},{9,8},{10,11... | collective-permute-start | bytes 38408 | tf_op jit(solution)/shard_map/ppermute | solution.py:370
  126.3 3.7 %collective-permute-start.18 = (f32[40,80]{1,0:T(8,128)S(1)}, f32[40,80]{1,0:T(8,128)S(1)}, u32[]{:S(2)}, u32[]{:S(2)}) collective-permute-start(f32[40,80]{1,0:T(8,128)S(1)} %add.41), channel_id=1, source_target_pairs={{0,2},{1,3},{2,0},{3,1},{4,6},{5,7},{6,4},{7,5},{8,10},{9,11},{10,... | collective-permute-start | bytes 38408 | tf_op jit(solution)/shard_map/ppermute | solution.py:370
  130.1 1.8 %collective-permute-done.18 = f32[40,80]{1,0:T(8,128)S(1)} collective-permute-done((f32[40,80]{1,0:T(8,128)S(1)}, f32[40,80]{1,0:T(8,128)S(1)}, u32[]{:S(2)}, u32[]{:S(2)}) %collective-permute-start.18) | collective-permute-done | bytes 12832 | tf_op jit(solution)/shard_map/ppermute | solution.py:370
  131.8 2.9 %collective-permute-done.19 = f32[40,80]{1,0:T(8,128)S(1)} collective-permute-done((f32[40,80]{1,0:T(8,128)S(1)}, f32[40,80]{1,0:T(8,128)S(1)}, u32[]{:S(2)}, u32[]{:S(2)}) %collective-permute-start.19) | collective-permute-done | bytes 12832 | tf_op jit(solution)/shard_map/ppermute | solution.py:370
  (47 shorter events, 14.2 us)
Async XLA Ops:
  0.6 4.7 %copy-start = (f32[16,8,1024]{2,1,0:T(8,128)S(1)}, f32[16,8,1024]{2,1,0:T(8,128)}, u32[]{:S(2)}) copy-start(f32[16,8,1024]{2,1,0:T(8,128)} %refs_3_.1) | copy-start | bytes 1572868
  0.6 4.7 %copy-start.1 = (f32[8,8,1024]{2,1,0:T(8,128)S(1)}, f32[8,8,1024]{2,1,0:T(8,128)}, u32[]{:S(2)}) copy-start(f32[8,8,1024]{2,1,0:T(8,128)} %refs_4_.1) | copy-start | bytes 786436
  2.3 5.2 %collective-permute-start = (f32[25,8,128]{2,1,0:T(8,128)}, f32[25,8,128]{2,1,0:T(8,128)S(1)}, u32[]{:S(2)}, u32[]{:S(2)}) collective-permute-start(f32[25,8,128]{2,1,0:T(8,128)} %get-tuple-element.22), channel_id=1, source_target_pairs={{0,64},{64,128},{128,192},{1,65},{65,129},{129,193},{2,66},{66,130... | collective-permute-start | bytes 307208 | tf_op jit(solution)/shard_map/ppermute | solution.py:379
  4.0 6.2 %collective-permute-start.1 = (f32[25,8,128]{2,1,0:T(8,128)}, f32[25,8,128]{2,1,0:T(8,128)S(1)}, u32[]{:S(2)}, u32[]{:S(2)}) collective-permute-start(f32[25,8,128]{2,1,0:T(8,128)} %get-tuple-element.23), channel_id=1, source_target_pairs={{64,0},{128,64},{192,128},{65,1},{129,65},{193,129},{66,2},{130,66... | collective-permute-start | bytes 307208 | tf_op jit(solution)/shard_map/ppermute | solution.py:380
  11.1 10.1 %collective-permute-start.2 = (f32[25,8,640]{2,1,0:T(8,128)S(1)}, f32[25,8,640]{2,1,0:T(8,128)S(1)}, u32[]{:S(2)}, u32[]{:S(2)}) collective-permute-start(f32[25,8,640]{2,1,0:T(8,128)S(1)} %get-tuple-element.25), channel_id=1, source_target_pairs={{0,1},{1,0},{2,3},{3,2},{4,5},{5,4},{6,7},{7,6},{8,9},{9,8},{10,11... | collective-permute-start | bytes 1536008 | tf_op jit(solution)/shard_map/ppermute | solution.py:370
  11.7 49.8 %collective-permute-start.3 = (f32[25,8,640]{2,1,0:T(8,128)S(1)}, f32[25,8,640]{2,1,0:T(8,128)S(1)}, u32[]{:S(2)}, u32[]{:S(2)}) collective-permute-start(f32[25,8,640]{2,1,0:T(8,128)S(1)} %get-tuple-element.24.keep_ref), channel_id=1, source_target_pairs={{0,2},{1,3},{2,4},{3,5},{4,6},{5,7},{6,8},{7,9},{8,10},{9,11},{10,... | collective-permute-start | bytes 1536008 | tf_op jit(solution)/shard_map/ppermute | solution.py:355
  15.6 45.9 %collective-permute-start.5 = (f32[25,8,640]{2,1,0:T(8,128)S(1)}, f32[25,8,640]{2,1,0:T(8,128)S(1)}, u32[]{:S(2)}, u32[]{:S(2)}) collective-permute-start(f32[25,8,640]{2,1,0:T(8,128)S(1)} %get-tuple-element.24.keep_ref), channel_id=1, source_target_pairs={{2,0},{3,1},{4,2},{5,3},{6,4},{7,5},{8,6},{9,7},{10,8},{11,9},{12,... | collective-permute-start | bytes 1536008 | tf_op jit(solution)/shard_map/ppermute | solution.py:355
  21.2 40.3 %collective-permute-start.4 = (f32[25,8,640]{2,1,0:T(8,128)S(1)}, f32[25,8,640]{2,1,0:T(8,128)S(1)}, u32[]{:S(2)}, u32[]{:S(2)}) collective-permute-start(f32[25,8,640]{2,1,0:T(8,128)S(1)} %collective-permute-done.2.give_ref), channel_id=1, source_target_pairs={{0,2},{1,3},{2,4},{3,5},{4,6},{5,7},{6,8},{7,9},{8,10},{9,11},{10,... | collective-permute-start | bytes 1536008 | tf_op jit(solution)/shard_map/ppermute | solution.py:355
  25.0 36.5 %collective-permute-start.6 = (f32[25,8,640]{2,1,0:T(8,128)S(1)}, f32[25,8,640]{2,1,0:T(8,128)S(1)}, u32[]{:S(2)}, u32[]{:S(2)}) collective-permute-start(f32[25,8,640]{2,1,0:T(8,128)S(1)} %collective-permute-done.2.give_ref), channel_id=1, source_target_pairs={{2,0},{3,1},{4,2},{5,3},{6,4},{7,5},{8,6},{9,7},{10,8},{11,9},{12,... | collective-permute-start | bytes 1536008 | tf_op jit(solution)/shard_map/ppermute | solution.py:355
  27.0 21.2 %collective-permute-start.7 = (f32[10,8,640]{2,1,0:T(8,128)S(1)}, f32[10,8,640]{2,1,0:T(8,128)S(1)}, u32[]{:S(2)}, u32[]{:S(2)}) collective-permute-start(f32[10,8,640]{2,1,0:T(8,128)S(1)} %get-tuple-element.26), channel_id=1, source_target_pairs={{1,5},{3,7},{4,0},{5,9},{6,2},{7,11},{8,4},{9,13},{10,6},{11,15},{... | collective-permute-start | bytes 614408 | tf_op jit(solution)/shard_map/ppermute | solution.py:361
  48.9 11.9 %collective-permute-start.8 = (f32[10,8,640]{2,1,0:T(8,128)S(1)}, f32[10,8,640]{2,1,0:T(8,128)S(1)}, u32[]{:S(2)}, u32[]{:S(2)}) collective-permute-start(f32[10,8,640]{2,1,0:T(8,128)S(1)} %get-tuple-element.27), channel_id=1, source_target_pairs={{1,4},{3,6},{4,1},{5,8},{6,3},{7,10},{8,5},{9,12},{10,7},{11,14},{... | collective-permute-start | bytes 614408 | tf_op jit(solution)/shard_map/ppermute | solution.py:361
  52.5 9.0 %copy-start.8 = (f32[16]{0:T(128)S(1)}, f32[16]{0:T(128)}, u32[]{:S(2)}) copy-start(f32[16]{0:T(128)} %stiff_ref.1) | copy-start | bytes 196
  52.5 9.0 %copy-start.9 = (f32[16]{0:T(128)S(1)}, f32[16]{0:T(128)}, u32[]{:S(2)}) copy-start(f32[16]{0:T(128)} %dens_ref.1) | copy-start | bytes 196
  90.2 9.0 %collective-permute-start.10 = (f32[40,80]{1,0:T(8,128)S(1)}, f32[40,80]{1,0:T(8,128)S(1)}, u32[]{:S(2)}, u32[]{:S(2)}) collective-permute-start(f32[40,80]{1,0:T(8,128)S(1)} %get-tuple-element.32), channel_id=1, source_target_pairs={{0,128},{64,192},{128,0},{192,64},{1,129},{65,193},{129,1},{193,65... | collective-permute-start | bytes 38408 | tf_op jit(solution)/shard_map/ppermute | solution.py:411
  94.6 6.1 %collective-permute-start.11 = (f32[40,80]{1,0:T(8,128)S(1)}, f32[40,80]{1,0:T(8,128)S(1)}, u32[]{:S(2)}, u32[]{:S(2)}) collective-permute-start(f32[40,80]{1,0:T(8,128)S(1)} %get-tuple-element.33), channel_id=1, source_target_pairs={{0,192},{64,0},{128,64},{192,128},{1,193},{65,1},{129,65},{193,129... | collective-permute-start | bytes 38408 | tf_op jit(solution)/shard_map/ppermute | solution.py:411
  99.2 4.7 %collective-permute-start.9 = (f32[40,80]{1,0:T(8,128)S(1)}, f32[40,80]{1,0:T(8,128)S(1)}, u32[]{:S(2)}, u32[]{:S(2)}) collective-permute-start(f32[40,80]{1,0:T(8,128)S(1)} %get-tuple-element.31), channel_id=1, source_target_pairs={{0,64},{64,128},{128,192},{192,0},{1,65},{65,129},{129,193},{193,1... | collective-permute-start | bytes 38408 | tf_op jit(solution)/shard_map/ppermute | solution.py:411
  103.9 19.6 %collective-permute-start.12 = (f32[24,8,512]{2,1,0:T(8,128)}, f32[24,8,512]{2,1,0:T(8,128)S(1)}, u32[]{:S(2)}, u32[]{:S(2)}) collective-permute-start(f32[24,8,512]{2,1,0:T(8,128)} %get-tuple-element.34), channel_id=1, source_target_pairs={{0,1},{1,0},{2,3},{3,2},{4,5},{5,4},{6,7},{7,6},{8,9},{9,8},{10,11... | collective-permute-start | bytes 1179656 | tf_op jit(solution)/shard_map/ppermute | solution.py:370
  104.0 4.8 %collective-permute-start.13 = (f32[40,80]{1,0:T(8,128)S(1)}, f32[40,80]{1,0:T(8,128)S(1)}, u32[]{:S(2)}, u32[]{:S(2)}) collective-permute-start(f32[40,80]{1,0:T(8,128)S(1)} %add_add_fusion.1), channel_id=1, source_target_pairs={{0,4},{1,5},{2,6},{3,7},{4,0},{5,1},{6,2},{7,3},{8,12},{9,13},{10,... | collective-permute-start | bytes 38408 | tf_op jit(solution)/shard_map/ppermute | solution.py:370
  108.8 5.9 %collective-permute-start.14 = (f32[40,80]{1,0:T(8,128)S(1)}, f32[40,80]{1,0:T(8,128)S(1)}, u32[]{:S(2)}, u32[]{:S(2)}) collective-permute-start(f32[40,80]{1,0:T(8,128)S(1)} %add.38), channel_id=1, source_target_pairs={{0,12},{1,13},{2,14},{3,15},{4,8},{5,9},{6,10},{7,11},{8,4},{9,5},... | collective-permute-start | bytes 38408 | tf_op jit(solution)/shard_map/ppermute | solution.py:370
  114.7 3.8 %collective-permute-start.15 = (f32[40,80]{1,0:T(8,128)S(1)}, f32[40,80]{1,0:T(8,128)S(1)}, u32[]{:S(2)}, u32[]{:S(2)}) collective-permute-start(f32[40,80]{1,0:T(8,128)S(1)} %add.39), channel_id=1, source_target_pairs={{0,16},{1,17},{2,18},{3,19},{4,20},{5,21},{6,22},{7,23},{8,24},{9,... | collective-permute-start | bytes 38408 | tf_op jit(solution)/shard_map/ppermute | solution.py:370
  118.5 5.0 %collective-permute-start.16 = (f32[40,80]{1,0:T(8,128)S(1)}, f32[40,80]{1,0:T(8,128)S(1)}, u32[]{:S(2)}, u32[]{:S(2)}) collective-permute-start(f32[40,80]{1,0:T(8,128)S(1)} %add.40), channel_id=1, source_target_pairs={{0,48},{1,49},{2,50},{3,51},{4,52},{5,53},{6,54},{7,55},{8,56},{9,... | collective-permute-start | bytes 38408 | tf_op jit(solution)/shard_map/ppermute | solution.py:370
  124.4 5.6 %collective-permute-start.17 = (f32[40,80]{1,0:T(8,128)S(1)}, f32[40,80]{1,0:T(8,128)S(1)}, u32[]{:S(2)}, u32[]{:S(2)}) collective-permute-start(f32[40,80]{1,0:T(8,128)S(1)} %add.41), channel_id=1, source_target_pairs={{0,1},{1,0},{2,3},{3,2},{4,5},{5,4},{6,7},{7,6},{8,9},{9,8},{10,11... | collective-permute-start | bytes 38408 | tf_op jit(solution)/shard_map/ppermute | solution.py:370
  126.3 5.5 %collective-permute-start.18 = (f32[40,80]{1,0:T(8,128)S(1)}, f32[40,80]{1,0:T(8,128)S(1)}, u32[]{:S(2)}, u32[]{:S(2)}) collective-permute-start(f32[40,80]{1,0:T(8,128)S(1)} %add.41), channel_id=1, source_target_pairs={{0,2},{1,3},{2,0},{3,1},{4,6},{5,7},{6,4},{7,5},{8,10},{9,11},{10,... | collective-permute-start | bytes 38408 | tf_op jit(solution)/shard_map/ppermute | solution.py:370
  130.1 4.7 %collective-permute-start.19 = (f32[40,80]{1,0:T(8,128)S(1)}, f32[40,80]{1,0:T(8,128)S(1)}, u32[]{:S(2)}, u32[]{:S(2)}) collective-permute-start(f32[40,80]{1,0:T(8,128)S(1)} %add.41), channel_id=1, source_target_pairs={{0,3},{1,2},{2,1},{3,0},{4,7},{5,6},{6,5},{7,4},{8,11},{9,10},{10,... | collective-permute-start | bytes 38408 | tf_op jit(solution)/shard_map/ppermute | solution.py:370
  (6 other events, 8.6 us)
where the time goes:
time: 136 us; the launch traced here: 135 us
  waiting for transfers between devices  54.2 us (40%)
  starting transfers between devices  44 us (32%)
  Pallas kernels  30.8 us (23%)
  local copies, waits for them, and re-layouts  3.88 us (3%)
  other arithmetic  1.6 us (1%)
    pallas_call x1, Pallas kernels, advance_block(): pl.pallas_call(wave_kernel, out_shape=(part, part) + (jax.ShapeDtypeStruc...  26.8 us
    ppermute x9, waiting for transfers between devices, swap(): return lax.ppermute(cells, 'dom', [(i, i ^ bit) for i in range(count)])  24.8 us
    ppermute x2, waiting for transfers between devices, outward(): lax.ppermute(cells, 'dom', [(i, j) for i, j in pairs if 0 <= j < count])  22 us
    ppermute x4, starting transfers between devices, along_dom(): lax.ppermute(cells, 'dom', [(i, i + distance) for i in range(count) if 0...  11.7 us
    ppermute x2, starting transfers between devices, outward(): lax.ppermute(cells, 'dom', [(i, j) for i, j in pairs if 0 <= j < count])  11.1 us
    ppermute x9, starting transfers between devices, swap(): return lax.ppermute(cells, 'dom', [(i, i ^ bit) for i in range(count)])  9.31 us
    ppermute x3, starting transfers between devices, body(): lax.ppermute(pieces[hop], 'sec', [(i, (i + hop) % sections) for i in rang...  8.96 us
    ppermute x3, waiting for transfers between devices, body(): lax.ppermute(pieces[hop], 'sec', [(i, (i + hop) % sections) for i in rang...  4.71 us
  transfers between devices with their start and end apart: 20, of which 12 were waited for; matrix products, arithmetic and copies ran while one was open for 0% of the time, Pallas kernels for 1%

commit v1 on v0

v1 whole, which is shorter than its diff:
```python
import math

import jax
import jax.numpy as jnp
from jax import lax
from jax.experimental import pallas as pl
from jax.experimental.pallas import tpu as pltpu
from jax.sharding import PartitionSpec as P


ROWS = 8
COLS = 1024
HALF = 512
LANES = 128
TILES = 5
WIDE = TILES * LANES
HALO = 20
ACT = 16
SENS = 8
RESP = ACT + SENS
SETS = RESP // 8
SNAPS = 10
STEPS = 20
REGIONS = 16
SLABS = ROWS * SETS + 1
NEAR = 3
FAR = NEAR * SETS + 1
OWN = 24
SHARE = 40
CELLS = 512 * 4096
FLAG_LANE = 112
ACT_SETS = ACT // 8
CENTRE_ROWS = 2 * ROWS
SENS_SLABS = ROWS + 1
ACT_SLABS = ROWS * ACT_SETS
ALL_ROWS = 64
DT = 0.35


def block_column(shape, dim):
    spot = lax.broadcasted_iota(jnp.int32, shape, dim)
    return (spot & (LANES - 1)) * TILES + (spot >> 7)


MATMUL = (((1,), (0,)), ((), ()))
FAST = dict(preferred_element_type=jnp.float32)
EXACT = dict(precision=lax.Precision.HIGHEST, preferred_element_type=jnp.float32)


def one_hot(hit):
    return jnp.where(hit, 1.0, 0.0).astype(jnp.bfloat16)


def halves(cells):
    high = cells.astype(jnp.bfloat16)
    return high, (cells - high.astype(jnp.float32)).astype(jnp.bfloat16)


def pick_columns(parts, pick):
    return sum(lax.dot_general(part, pick, MATMUL, **FAST) for part in parts)


def turn_rows(parts, turn):
    return [lax.dot_general(turn, part, MATMUL, **FAST).astype(jnp.bfloat16) for part in parts]


def row_major(count=RESP, inverse=False):
    shape = (ROWS * count, ROWS * count)
    old = lax.broadcasted_iota(jnp.int32, shape, 0 if inverse else 1)
    new = lax.broadcasted_iota(jnp.int32, shape, 1 if inverse else 0)
    return one_hot(new == (old & (ROWS - 1)) * count + (old >> 3))


def edge_kernel(*refs):
    for act_ref, sens_ref, ids_ref, out_ref in (refs[0:3] + refs[6:7], refs[3:6] + refs[7:8]):
        out_ref[0:ACT] = act_ref[...]
        out_ref[ACT:RESP] = sens_ref[...]
        out_ref[RESP] = ids_ref[...].astype(jnp.float32) + 1.0


def edges(actuator_fields, sensor_fields, region_ids):
    def blocks(column):
        return [
            pl.BlockSpec((ACT, ROWS, LANES), lambda i, c=column: (0, 0, c)),
            pl.BlockSpec((SENS, ROWS, LANES), lambda i, c=column: (0, 0, c)),
            pl.BlockSpec((ROWS, LANES), lambda i, c=column: (0, c)),
        ]

    out = jax.ShapeDtypeStruct((RESP + 1, ROWS, LANES), jnp.float32)
    whole = pl.BlockSpec((RESP + 1, ROWS, LANES), lambda i: (0, 0, 0))
    fields = (actuator_fields, sensor_fields, region_ids)
    return pl.pallas_call(
        edge_kernel,
        grid=(1,),
        out_shape=(out, out),
        in_specs=blocks(COLS // LANES - 1) + blocks(0),
        out_specs=(whole, whole),
    )(*fields, *fields)


def main_kernel(act_ref, sens_ref, ids_ref, sup_ref, first_ref, second_ref):
    turn = row_major()
    cells = jnp.concatenate(
        [act_ref[...].reshape(ACT * ROWS, COLS), sens_ref[...].reshape(SENS * ROWS, COLS)], axis=0
    )
    parts = turn_rows(halves(cells), turn)
    ids = (ids_ref[...].astype(jnp.float32) + 1.0).astype(jnp.bfloat16)
    shape = (WIDE, WIDE)
    column = block_column(shape, 1)
    source = lax.broadcasted_iota(jnp.int32, shape, 0)
    inner = column < HALF + HALO
    outer = column >= WIDE - HALO
    for out_ref, begin, wanted in (
        (first_ref, 0, jnp.where(inner, column, -1)),
        (second_ref, COLS - WIDE, jnp.where(column < HALF, column + LANES, jnp.where(outer, column - HALF, -1))),
    ):
        pick = one_hot(source == wanted)
        cut = slice(begin, begin + WIDE)
        out_ref[0 : SLABS - 1] = pick_columns([part[:, cut] for part in parts], pick).reshape(SLABS - 1, 8, WIDE)
        out_ref[SLABS - 1] = pick_columns([ids[:, cut]], pick)
        out_ref[SLABS - 1, :, FLAG_LANE : FLAG_LANE + SNAPS] = sup_ref[...].astype(jnp.float32)


def halo_kernel(side_ref, first_ref, second_ref, left_ref, right_ref, *out_refs):
    turn = row_major()
    shape = (LANES, WIDE)
    column = block_column(shape, 1)
    source = lax.broadcasted_iota(jnp.int32, shape, 0)
    blocks = []
    for in_ref, edge_ref, hit in (
        (first_ref, left_ref, (column >= WIDE - HALO) & (source == column - HALF)),
        (second_ref, right_ref, (column >= HALF) & (column < HALF + HALO) & (source == column - HALF)),
    ):
        pick = one_hot(hit)
        parts = turn_rows(halves(edge_ref[0:RESP].reshape(RESP * ROWS, LANES)), turn)
        fields = in_ref[0 : SLABS - 1] + pick_columns(parts, pick).reshape(SLABS - 1, 8, WIDE)
        ids = in_ref[SLABS - 1] + pick_columns([edge_ref[RESP].astype(jnp.bfloat16)], pick)
        blocks.append((fields, ids))
    low_side = side_ref[0] == 0
    (fields_0, ids_0), (fields_1, ids_1) = blocks
    near = NEAR * SETS
    keep_s_ref, keep_a_ref, give_ref, far_keep_ref, far_give_ref = out_refs
    for sens_ref, act_ref, far_ref, fields, ids in (
        (keep_s_ref, keep_a_ref, far_keep_ref, jnp.where(low_side, fields_0, fields_1), jnp.where(low_side, ids_0, ids_1)),
        (
            give_ref.at[0:SENS_SLABS], give_ref.at[SENS_SLABS:], far_give_ref,
            jnp.where(low_side, fields_1, fields_0), jnp.where(low_side, ids_1, ids_0),
        ),
    ):
        grid = fields.reshape(ROWS, SETS, 8, WIDE)
        act_ref[...] = grid[:, :ACT_SETS].reshape(ACT_SLABS, 8, WIDE)
        sens_ref[0:ROWS] = grid[:, ACT_SETS]
        sens_ref[ROWS] = ids
        far_ref[0:near] = jnp.where(low_side, fields[:near], fields[SLABS - 1 - near :])
        far_ref[near] = ids


def after(cells):
    return jnp.concatenate([cells[:, LANES:], pltpu.roll(cells[:, :LANES], LANES - 1, 1)], axis=1)


def strip_bases(side):
    return [OWN + shift + spot for shift in (0, -16, 16) for spot in (8 * side, 8 - 8 * side)]


def fill(side, strips, far, sets, offset, p_ref, u_ref, mk_ref):
    def place(slab, row, spot):
        begin = slab * (mk_ref[row] * (DT / (0.5 * DT * DT)))
        u_ref[spot] = begin
        p_ref[spot] = begin

    for ref, base in zip(strips, strip_bases(side)):
        def fill_row(row, carry, ref=ref, base=base):
            for index in range(sets):
                place(ref[row * sets + index], base + row, (base + row) * sets + index)
            return carry

        lax.fori_loop(0, ROWS, fill_row, 0)
    for ref, above in zip(far, (side, 1 - side)):
        base = above * (8 - NEAR) + (ALL_ROWS - 8) * (1 - above)
        for row in range(NEAR):
            for index in range(sets):
                place(ref[row * SETS + offset + index], base + row, (base + row) * sets + index)


def step(count, sets, unroll, p_ref, u_ref, fx_ref, fy_ref, fw_ref, mk_ref):
    first = OWN - STEPS + 1 + count
    rows = CENTRE_ROWS + 2 * (STEPS - 1) - 2 * count

    def start(index):
        centre = p_ref[first * sets + index]
        north = fx_ref[first] * (centre - p_ref[(first - 1) * sets + index])
        return centre, north

    def one(row, carry):
        face = fx_ref[row + 1]
        along = fy_ref[row]
        back = fw_ref[row]
        mass = mk_ref[row]
        done = []
        for index, (centre, north) in enumerate(carry):
            spot = row * sets + index
            below = p_ref[spot + sets]
            south = face * (below - centre)
            east = along * (after(centre) - centre)
            first_west = back * (centre[:, :LANES] - pltpu.roll(centre[:, WIDE - LANES :], 1, 1))
            west = jnp.concatenate([first_west, east[:, : WIDE - LANES]], axis=1)
            speed = u_ref[spot] + mass * ((south - north) + (east - west))
            u_ref[spot] = speed
            p_ref[spot] = centre + speed
            done.append((below, south))
        return tuple(done)

    def several(turn, carry):
        row = first + unroll * turn
        for extra in range(unroll):
            carry = one(row + extra, carry)
        return carry

    lax.fori_loop(0, (rows + unroll - 1) // unroll, several, tuple(start(index) for index in range(sets)))


def march(sets, unroll, keep_row, mask_ref, p_ref, u_ref, *faces):
    def snapshot(index):
        for strip in range(2):
            mask = jnp.broadcast_to(mask_ref[strip, pl.ds(index, 1), :], (8, WIDE))
            fast = mask * (1.0 / DT)

            def keep_rows(turn, carry, strip=strip, mask=mask, fast=fast):
                for extra in range(4):
                    at = turn * 4 + extra + 8 * strip
                    keep_row(index, at, (OWN + at) * sets, mask, fast)
                return carry

            lax.fori_loop(0, 2, keep_rows, 0)

    def advance(index, carry):
        step(2 * index, sets, unroll, p_ref, u_ref, *faces)
        step(2 * index + 1, sets, unroll, p_ref, u_ref, *faces)
        snapshot(index)
        return carry

    step(1, sets, unroll, p_ref, u_ref, *faces)
    snapshot(0)
    lax.fori_loop(1, SNAPS, advance, 0)


def in_order(side, sets, p_ref):
    shape = (WIDE, HALF)
    pick = one_hot(lax.broadcasted_iota(jnp.int32, shape, 1) == block_column(shape, 0))
    turn = row_major(8 * sets, inverse=True)
    for base in strip_bases(side)[:2]:
        cells = p_ref[pl.ds(base * sets, ROWS * sets)].reshape(ROWS * 8 * sets, WIDE)
        yield pick_columns(turn_rows(halves(cells), turn), pick).reshape(8 * sets, ROWS, HALF)


def sensor_kernel(
    side_ref, stiff_ref, dens_ref,
    keep_ref, give_ref, up_ref, dn_ref, far_keep_ref, far_give_ref,
    own_ref, other_ref, frames_ref, fx_ref, fy_ref, fw_ref, mk_ref, mask_ref,
    p_ref, u_ref, s_ref, m_ref, fs_ref,
):
    side = side_ref[0]
    strips = [keep_ref, give_ref.at[0:SENS_SLABS]]
    for ref in (up_ref, dn_ref):
        strips += [ref.at[0:SENS_SLABS], ref.at[SENS_SLABS:]]
    far = (far_keep_ref, far_give_ref)

    def materials(ids, base):
        stiff = jnp.zeros_like(ids)
        dens = jnp.zeros_like(ids)
        for region in range(REGIONS):
            here = ids == region + 1.0
            stiff = jnp.where(here, stiff_ref[region], stiff)
            dens = jnp.where(here, dens_ref[region], dens)
        inside = ids > 0.0
        rows = pl.ds(pl.multiple_of(base, 8), 8)
        s_ref[rows, :] = stiff
        m_ref[rows, :] = jnp.where(inside, (0.5 * DT * DT) / jnp.where(inside, dens, 1.0), 0.0)

    for ref, base in zip(strips, strip_bases(side)):
        materials(ref[ROWS], base)
    for ref, above in zip(far, (side, 1 - side)):
        materials(ref[FAR - 1], (ALL_ROWS - 8) * (1 - above))
    shape = (8, WIDE)
    tile = 4 * side + (block_column(shape, 1) >> 7)
    inside = block_column(shape, 1) < HALF
    spread = one_hot(inside & (lax.broadcasted_iota(jnp.int32, shape, 0) == tile))
    for ref, strip in ((keep_ref, side), (give_ref, 1 - side)):
        flags = ref[ROWS, :, 0:LANES].astype(jnp.bfloat16)
        masks = lax.dot_general(flags, spread, (((0,), (0,)), ((), ())), **FAST)
        mask_ref[strip] = masks[FLAG_LANE:LANES]

    def coefficients(turn, carry):
        for extra in range(9):
            row = 1 + turn * 9 + extra
            centre = jnp.broadcast_to(s_ref[pl.ds(row, 1), :], (8, WIDE))
            upper = jnp.broadcast_to(s_ref[pl.ds(row - 1, 1), :], (8, WIDE))
            fx_ref[row] = centre + upper
            fy_ref[row] = centre + after(centre)
            fw_ref[row] = centre[:, :LANES] + pltpu.roll(centre[:, WIDE - LANES :], 1, 1)
            mk_ref[row] = jnp.broadcast_to(m_ref[pl.ds(row, 1), :], (8, WIDE))
        return carry

    lax.fori_loop(0, (ALL_ROWS - 1) // 9, coefficients, 0)
    fill(side, strips, far, 1, ACT_SETS, p_ref, u_ref, mk_ref)

    def keep_row(index, at, spot, mask, fast):
        rows = pl.ds(pl.multiple_of(index * SENS, SENS), SENS)
        fs_ref[at, rows, 0:WIDE] = p_ref[spot] * mask
        fs_ref[at, rows, WIDE : 2 * WIDE] = u_ref[spot] * fast

    march(1, 8, keep_row, mask_ref, p_ref, u_ref, fx_ref, fy_ref, fw_ref, mk_ref)

    def narrow(row, carry):
        frames_ref[row] = fs_ref[row].astype(jnp.bfloat16)
        return carry

    lax.fori_loop(0, CENTRE_ROWS, narrow, 0)
    for out_ref, cells in zip((own_ref, other_ref), in_order(side, 1, p_ref)):
        out_ref[...] = cells


def actuator_kernel(
    side_ref, place_ref,
    keep_ref, give_ref, up_ref, dn_ref, far_keep_ref, far_give_ref,
    own_sens_ref, other_sens_ref, frames_ref, fx_ref, fy_ref, fw_ref, mk_ref, mask_ref,
    own_ref, other_ref, piece_0_ref, piece_1_ref, piece_2_ref, piece_3_ref,
    p_ref, u_ref, fa_ref, acc_ref,
):
    side = side_ref[0]
    strips = [keep_ref, give_ref.at[SENS_SLABS:]]
    for ref in (up_ref, dn_ref):
        strips += [ref.at[0:ACT_SLABS], ref.at[ACT_SLABS:]]
    fill(side, strips, (far_keep_ref, far_give_ref), ACT_SETS, 0, p_ref, u_ref, mk_ref)

    def keep_row(index, at, spot, mask, fast):
        rows = pl.ds(pl.multiple_of(index * ACT, ACT), ACT)
        place = jnp.concatenate([p_ref[spot] * mask, p_ref[spot + 1] * mask], axis=0)
        speed = jnp.concatenate([u_ref[spot] * fast, u_ref[spot + 1] * fast], axis=0)
        fa_ref[at, rows, 0:WIDE] = place.astype(jnp.bfloat16)
        fa_ref[at, rows, WIDE : 2 * WIDE] = speed.astype(jnp.bfloat16)

    march(ACT_SETS, 6, keep_row, mask_ref, p_ref, u_ref, fx_ref, fy_ref, fw_ref, mk_ref)

    def gram(turn, total):
        for extra in range(4):
            row = 4 * turn + extra
            total = total + lax.dot_general(fa_ref[row], frames_ref[row], (((1,), (1,)), ((), ())), **FAST)
        return total

    total = lax.fori_loop(0, CENTRE_ROWS // 4, gram, jnp.zeros((ACT * SNAPS, SENS * SNAPS), jnp.float32))
    shape = (ACT * SNAPS, ACT * SNAPS)
    old = lax.broadcasted_iota(jnp.int32, shape, 1)
    new = lax.broadcasted_iota(jnp.int32, shape, 0)
    turn = jnp.where(new == (old & (ACT - 1)) * SNAPS + (old >> 4), 1.0, 0.0)
    shape = (SENS * SNAPS, SENS * SNAPS)
    old = lax.broadcasted_iota(jnp.int32, shape, 0)
    new = lax.broadcasted_iota(jnp.int32, shape, 1)
    turn_back = jnp.where(new == (old & (SENS - 1)) * SNAPS + (old >> 3), 1.0, 0.0)
    turned = lax.dot_general(turn, total, MATMUL, **EXACT)
    acc_ref[...] = lax.dot_general(turned, turn_back, MATMUL, **EXACT) * (1.0 / math.sqrt(CELLS))
    place = place_ref[0]
    for hop, out_ref in enumerate((piece_0_ref, piece_1_ref, piece_2_ref, piece_3_ref)):
        out_ref[...] = acc_ref[pl.ds(pl.multiple_of(((place + hop) & 3) * SHARE, 8), SHARE), :]
    for out_ref, cells, sens_ref in zip(
        (own_ref, other_ref), in_order(side, ACT_SETS, p_ref), (own_sens_ref, other_sens_ref)
    ):
        out_ref[0:ACT] = cells
        out_ref[ACT:RESP] = sens_ref[...]


def array(*shape, dtype=jnp.float32):
    return jax.ShapeDtypeStruct(shape, dtype)


def scratch(*shape, dtype=jnp.float32):
    return pltpu.VMEM(shape, dtype)


def call(kernel, scalars, operands, out_shape, scratch_shapes, mebibytes):
    vmem = pl.BlockSpec(memory_space=pltpu.VMEM)
    smem = pl.BlockSpec(memory_space=pltpu.SMEM)
    return pl.pallas_call(
        kernel,
        out_shape=out_shape,
        in_specs=[smem] * len(scalars) + [vmem] * len(operands),
        out_specs=(vmem,) * len(out_shape),
        scratch_shapes=scratch_shapes,
        compiler_params=grant(mebibytes),
    )(*scalars, *operands)


def sensor_block(scalars, operands):
    face = array(ALL_ROWS, 8, WIDE)
    part = array(SENS, ROWS, HALF)
    return call(
        sensor_kernel, scalars, operands,
        (
            part, part, array(CENTRE_ROWS, SENS * SNAPS, 2 * WIDE, dtype=jnp.bfloat16),
            face, face, array(ALL_ROWS, 8, LANES), face, array(2, LANES - FLAG_LANE, WIDE),
        ),
        [
            scratch(ALL_ROWS, 8, WIDE), scratch(ALL_ROWS, 8, WIDE), scratch(ALL_ROWS, WIDE), scratch(ALL_ROWS, WIDE),
            scratch(CENTRE_ROWS, SENS * SNAPS, 2 * WIDE),
        ],
        28,
    )


def actuator_block(scalars, operands):
    part = array(RESP, ROWS, HALF)
    state = scratch(ALL_ROWS * ACT_SETS, 8, WIDE)
    return call(
        actuator_kernel, scalars, operands,
        (part, part) + (array(SHARE, SENS * SNAPS),) * 4,
        [
            state, state,
            scratch(CENTRE_ROWS, ACT * SNAPS, 2 * WIDE, dtype=jnp.bfloat16),
            scratch(ACT * SNAPS, SENS * SNAPS),
        ],
        36,
    )


def along_dom(cells, distance):
    count = lax.axis_size("dom")
    return lax.ppermute(cells, "dom", [(i, i + distance) for i in range(count) if 0 <= i + distance < count])


def outward(cells, distance):
    count = lax.axis_size("dom")
    pairs = [(i, i + distance if i % 2 else i - distance) for i in range(count)]
    return lax.ppermute(cells, "dom", [(i, j) for i, j in pairs if 0 <= j < count])


def grant(mebibytes):
    return pltpu.CompilerParams(vmem_limit_bytes=mebibytes << 20)


def swap(cells, bit):
    count = lax.axis_size("dom")
    return lax.ppermute(cells, "dom", [(i, i ^ bit) for i in range(count)])


def body(actuator_fields, sensor_fields, region_ids, stiffness_table, density_table, supported):
    side = lax.axis_index("dom") % 2
    side_word = side.astype(jnp.int32).reshape(1)
    place_word = lax.axis_index("sec").astype(jnp.int32).reshape(1)
    sections = lax.axis_size("sec")
    right_edge, left_edge = edges(actuator_fields, sensor_fields, region_ids)
    left = lax.ppermute(right_edge, "sec", [(i, i + 1) for i in range(sections - 1)])
    right = lax.ppermute(left_edge, "sec", [(i + 1, i) for i in range(sections - 1)])
    flags = jnp.transpose(supported, (1, 2, 0)).reshape(-1, SNAPS)

    vmem = pl.BlockSpec(memory_space=pltpu.VMEM)
    smem = pl.BlockSpec(memory_space=pltpu.SMEM)
    block = jax.ShapeDtypeStruct((SLABS, 8, WIDE), jnp.float32)
    first, second = pl.pallas_call(
        main_kernel, out_shape=(block, block), in_specs=[vmem] * 4, out_specs=(vmem, vmem), compiler_params=grant(16)
    )(actuator_fields, sensor_fields, region_ids, flags)
    far = array(FAR, 8, WIDE)
    outs = (array(SENS_SLABS, 8, WIDE), array(ACT_SLABS, 8, WIDE), block, far, far)
    keep_s, keep_a, give, far_keep, far_give = call(halo_kernel, (side_word,), (first, second, left, right), outs, [], 16)

    far_keep = outward(far_keep, 4)
    got = swap(give, 1)
    far_give = outward(far_give, 3)
    both_s = jnp.concatenate([keep_s, got[:SENS_SLABS]], 0)
    up_s = along_dom(both_s, 2)
    dn_s = along_dom(both_s, -2)
    both_a = jnp.concatenate([keep_a, got[SENS_SLABS:]], 0)
    up_a = along_dom(both_a, 2)
    dn_a = along_dom(both_a, -2)
    far = (far_keep, far_give)
    sensor = sensor_block((side_word, stiffness_table, density_table), (keep_s, got, up_s, dn_s) + far)
    own, other, *pieces = actuator_block((side_word, place_word), (keep_a, got, up_a, dn_a) + far + tuple(sensor))
    total = pieces[0]
    for hop in range(1, sections):
        total = total + lax.ppermute(pieces[hop], "sec", [(i, (i + hop) % sections) for i in range(sections)])
    other, total = lax.optimization_barrier((other, total))
    back = swap(other, 1)
    position = jnp.where(
        side == 0, jnp.concatenate([own, back], 2), jnp.concatenate([back, own], 2)
    )
    for bits in (4, 12, 16, 48):
        total = total + swap(total, bits)
    position, total = lax.optimization_barrier((position, total))
    total = total + sum(swap(total, bits) for bits in (1, 2, 3))
    return (position, total)


def solution(mesh):
    in_specs = (
        P(None, "dom", "sec"),
        P(None, "dom", "sec"),
        P("dom", "sec"),
        P(),
        P(),
        P(None, "dom", "sec"),
    )
    out_specs = (P(None, "dom", "sec"), P("sec", None))
    return jax.shard_map(body, mesh=mesh, in_specs=in_specs, out_specs=out_specs, check_vma=False)
```

time: 136 us -> 142 us (1.044)
  the two profiles are of different devices: /device:TPU:56 before, /device:TPU:24 now
where the time goes in v1:
time: 142 us
  waiting for transfers between devices  55.8 us (39%)
  starting transfers between devices  46.7 us (33%)
  Pallas kernels  35.5 us (25%)
  other arithmetic  3.25 us (2%)
    pallas_call x3, Pallas kernels, call(): pl.pallas_call(kernel, out_shape=out_shape, in_specs=[smem] * len(scalars...  32.3 us
    ppermute x9, waiting for transfers between devices, swap(): return lax.ppermute(cells, 'dom', [(i, i ^ bit) for i in range(count)])  26.6 us
    ppermute x2, waiting for transfers between devices, outward(): lax.ppermute(cells, 'dom', [(i, j) for i, j in pairs if 0 <= j < count])  21.5 us
    ppermute x4, starting transfers between devices, along_dom(): lax.ppermute(cells, 'dom', [(i, i + distance) for i in range(count) if 0...  17.8 us
    ppermute x9, starting transfers between devices, swap(): return lax.ppermute(cells, 'dom', [(i, i ^ bit) for i in range(count)])  11.8 us
    ppermute x3, starting transfers between devices, body(): lax.ppermute(pieces[hop], 'sec', [(i, (i + hop) % sections) for i in rang...  7.73 us
    ppermute x2, starting transfers between devices, outward(): lax.ppermute(cells, 'dom', [(i, j) for i, j in pairs if 0 <= j < count])  6.26 us
    ppermute x3, waiting for transfers between devices, body(): lax.ppermute(pieces[hop], 'sec', [(i, (i + hop) % sections) for i in rang...  4.36 us
  transfers between devices with their start and end apart: 20, of which 13 were waited for; matrix products, arithmetic and copies ran while one was open for 1% of the time, Pallas kernels for 10%

profile of v1, /device:TPU:24, one launch (start us, length us, event | category | flops | bytes accessed | tf_op | source)
XLA Modules:
  0.0 142.2 jit_solution(14277235351180716640)
XLA Ops:
  0.7 1.7 %shard_map.78 = (f32[25,8,128]{2,1,0:T(8,128)}, f32[25,8,128]{2,1,0:T(8,128)}) custom-call(f32[16,8,1024]{2,1,0:T(8,128)} %refs_3_.1, f32[8,8,1024]{2,1,0:T(8,128)} %refs_4_.1, s32[8,1024]{1,0:T(8,128)} %refs_5_.1, f32[16,8,1024]{2,1,0:T(8,128)} %refs_3_.1, f32[8,8,1024]{2,1,0:T(8,128)} %refs_4_.1, s32[8,1024]{1,0:T(8,128)} %refs_5_.1), custom_call_target="tpu_custom_call" | custom-call | tf_op jit(solution)/shard_map/pallas_call | solution.py:92
  2.3 1.7 %collective-permute-start = (f32[25,8,128]{2,1,0:T(8,128)}, f32[25,8,128]{2,1,0:T(8,128)S(1)}, u32[]{:S(2)}, u32[]{:S(2)}) collective-permute-start(f32[25,8,128]{2,1,0:T(8,128)} %get-tuple-element.31), channel_id=1, source_target_pairs={{0,64},{64,128},{128,192},{1,65},{65,129},{129,193},{2,66},{66,130... | collective-permute-start | bytes 307208 | tf_op jit(solution)/shard_map/ppermute | solution.py:452
  5.4 1.5 %shard_map.77 = (f32[25,8,640]{2,1,0:T(8,128)S(1)}, f32[25,8,640]{2,1,0:T(8,128)S(1)}) custom-call(f32[16,8,1024]{2,1,0:T(8,128)S(1)} %copy-done, f32[8,8,1024]{2,1,0:T(8,128)S(1)} %copy-done.1, s32[8,1024]{1,0:T(8,128)S(1)} %copy-done.2, s32[8,10]{1,0:T(8,128)S(1)} %bitcast.5), custom_call_target="tpu_custom_call" | custom-call | tf_op jit(solution)/shard_map/pallas_call | solution.py:459
  6.9 3.4 %collective-permute-done.1.right_ref = f32[25,8,128]{2,1,0:T(8,128)S(1)} collective-permute-done((f32[25,8,128]{2,1,0:T(8,128)}, f32[25,8,128]{2,1,0:T(8,128)S(1)}, u32[]{:S(2)}, u32[]{:S(2)}) %collective-permute-start.1) | collective-permute-done | bytes 102432 | tf_op jit(solution)/shard_map/ppermute | solution.py:453
  12.3 9.4 %collective-permute-done.2.give_ref = f32[25,8,640]{2,1,0:T(8,128)S(1)} collective-permute-done((f32[25,8,640]{2,1,0:T(8,128)S(1)}, f32[25,8,640]{2,1,0:T(8,128)S(1)}, u32[]{:S(2)}, u32[]{:S(2)}) %collective-permute-start.2) | collective-permute-done | bytes 512032 | tf_op jit(solution)/shard_map/ppermute | solution.py:443
  22.7 3.8 %collective-permute-start.3 = (f32[32,8,640]{2,1,0:T(8,128)}, f32[32,8,640]{2,1,0:T(8,128)S(1)}, u32[]{:S(2)}, u32[]{:S(2)}) collective-permute-start(f32[32,8,640]{2,1,0:T(8,128)} %pad_maximum_fusion), channel_id=1, source_target_pairs={{0,2},{1,3},{2,4},{3,5},{4,6},{5,7},{6,8},{7,9},{8,10},{9,11},{10,... | collective-permute-start | bytes 1966088 | tf_op jit(solution)/shard_map/ppermute | solution.py:428
  26.5 6.1 %collective-permute-start.4 = (f32[32,8,640]{2,1,0:T(8,128)}, f32[32,8,640]{2,1,0:T(8,128)S(1)}, u32[]{:S(2)}, u32[]{:S(2)}) collective-permute-start(f32[32,8,640]{2,1,0:T(8,128)} %pad_maximum_fusion), channel_id=1, source_target_pairs={{2,0},{3,1},{4,2},{5,3},{6,4},{7,5},{8,6},{9,7},{10,8},{11,9},{12,... | collective-permute-start | bytes 1966088 | tf_op jit(solution)/shard_map/ppermute | solution.py:428
  32.5 4.3 %collective-permute-start.5 = (f32[10,8,640]{2,1,0:T(8,128)S(1)}, f32[10,8,640]{2,1,0:T(8,128)S(1)}, u32[]{:S(2)}, u32[]{:S(2)}) collective-permute-start(f32[10,8,640]{2,1,0:T(8,128)S(1)} %get-tuple-element.35), channel_id=1, source_target_pairs={{1,5},{3,7},{4,0},{5,9},{6,2},{7,11},{8,4},{9,13},{10,6},{11,15},{... | collective-permute-start | bytes 614408 | tf_op jit(solution)/shard_map/ppermute | solution.py:434
  37.7 2.9 %collective-permute-start.7 = (f32[18,8,640]{2,1,0:T(8,128)}, f32[18,8,640]{2,1,0:T(8,128)S(1)}, u32[]{:S(2)}, u32[]{:S(2)}) collective-permute-start(f32[18,8,640]{2,1,0:T(8,128)} %pad_maximum_fusion.1), channel_id=1, source_target_pairs={{0,2},{1,3},{2,4},{3,5},{4,6},{5,7},{6,8},{7,9},{8,10},{9,11},{10,... | collective-permute-start | bytes 1105928 | tf_op jit(solution)/shard_map/ppermute | solution.py:428
  40.6 5.0 %collective-permute-start.8 = (f32[18,8,640]{2,1,0:T(8,128)}, f32[18,8,640]{2,1,0:T(8,128)S(1)}, u32[]{:S(2)}, u32[]{:S(2)}) collective-permute-start(f32[18,8,640]{2,1,0:T(8,128)} %pad_maximum_fusion.1), channel_id=1, source_target_pairs={{2,0},{3,1},{4,2},{5,3},{6,4},{7,5},{8,6},{9,7},{10,8},{11,9},{12,... | collective-permute-start | bytes 1105928 | tf_op jit(solution)/shard_map/ppermute | solution.py:428
  45.6 5.3 %collective-permute-done.5.far_keep_ref = f32[10,8,640]{2,1,0:T(8,128)S(1)} collective-permute-done((f32[10,8,640]{2,1,0:T(8,128)S(1)}, f32[10,8,640]{2,1,0:T(8,128)S(1)}, u32[]{:S(2)}, u32[]{:S(2)}) %collective-permute-start.5) | collective-permute-done | bytes 204832 | tf_op jit(solution)/shard_map/ppermute | solution.py:434
  50.9 1.9 %collective-permute-start.6 = (f32[10,8,640]{2,1,0:T(8,128)}, f32[10,8,640]{2,1,0:T(8,128)S(1)}, u32[]{:S(2)}, u32[]{:S(2)}) collective-permute-start(f32[10,8,640]{2,1,0:T(8,128)} %get-tuple-element.36), channel_id=1, source_target_pairs={{1,4},{3,6},{4,1},{5,8},{6,3},{7,10},{8,5},{9,12},{10,7},{11,14},{... | collective-permute-start | bytes 614408 | tf_op jit(solution)/shard_map/ppermute | solution.py:434
  52.8 16.3 %collective-permute-done.6.far_give_ref = f32[10,8,640]{2,1,0:T(8,128)S(1)} collective-permute-done((f32[10,8,640]{2,1,0:T(8,128)}, f32[10,8,640]{2,1,0:T(8,128)S(1)}, u32[]{:S(2)}, u32[]{:S(2)}) %collective-permute-start.6) | collective-permute-done | bytes 204832 | tf_op jit(solution)/shard_map/ppermute | solution.py:434
  69.1 12.9 %shard_map.80 = (f32[8,8,512]{2,1,0:T(8,128)S(1)}, f32[8,8,512]{2,1,0:T(8,128)S(1)}, bf16[16,80,1280]{2,1,0:T(8,128)(2,1)S(1)}, f32[64,8,640]{2,1,0:T(8,128)S(1)...) custom-call(s32[1]{0:T(128)} %bitcast.side_ref, ...), custom_call_target="tpu_custom_call" | custom-call | tf_op jit(solution)/shard_map/pallas_call | solution.py:384
  82.0 18.0 %shard_map.81 = (f32[24,8,512]{2,1,0:T(8,128)S(1)}, f32[24,8,512]{2,1,0:T(8,128)S(1)}, f32[40,80]{1,0:T(8,128)S(1)}, f32[40,80]{1,0:T(8,128)S(1)}, f32[40,80]{1,0:T(8,128)S(1)}, /*index=5*/f32[40,80]{1,0:T(8,128)S(1)}) custom-call(s32[1]{0:T(128)} %bitcast.side_ref, s32[1]{0:T(128)} %bitcast.1.place_ref, f32[16,8,640]{2,1,0:T(8,128)S(1)} %get-tuple-element.33.keep_ref, ...), custom_call_target="tpu_custom_call" | custom-call | tf_op jit(solution)/shard_map/pallas_call | solution.py:384
  100.0 7.2 %collective-permute-start.10 = (f32[40,80]{1,0:T(8,128)S(1)}, f32[40,80]{1,0:T(8,128)S(1)}, u32[]{:S(2)}, u32[]{:S(2)}) collective-permute-start(f32[40,80]{1,0:T(8,128)S(1)} %get-tuple-element.50), channel_id=1, source_target_pairs={{0,128},{64,192},{128,0},{192,64},{1,129},{65,193},{129,1},{193,65... | collective-permute-start | bytes 38408 | tf_op jit(solution)/shard_map/ppermute | solution.py:480
  109.1 3.0 %collective-permute-done.9 = f32[40,80]{1,0:T(8,128)S(1)} collective-permute-done((f32[40,80]{1,0:T(8,128)S(1)}, f32[40,80]{1,0:T(8,128)S(1)}, u32[]{:S(2)}, u32[]{:S(2)}) %collective-permute-start.9) | collective-permute-done | bytes 12832 | tf_op jit(solution)/shard_map/ppermute | solution.py:480
  112.8 5.9 %collective-permute-start.13 = (f32[40,80]{1,0:T(8,128)S(1)}, f32[40,80]{1,0:T(8,128)S(1)}, u32[]{:S(2)}, u32[]{:S(2)}) collective-permute-start(f32[40,80]{1,0:T(8,128)S(1)} %add_add_fusion.1), channel_id=1, source_target_pairs={{0,4},{1,5},{2,6},{3,7},{4,0},{5,1},{6,2},{7,3},{8,12},{9,13},{10,... | collective-permute-start | bytes 38408 | tf_op jit(solution)/shard_map/ppermute | solution.py:443
  118.7 1.8 %collective-permute-done.13 = f32[40,80]{1,0:T(8,128)S(1)} collective-permute-done((f32[40,80]{1,0:T(8,128)S(1)}, f32[40,80]{1,0:T(8,128)S(1)}, u32[]{:S(2)}, u32[]{:S(2)}) %collective-permute-start.13) | collective-permute-done | bytes 12832 | tf_op jit(solution)/shard_map/ppermute | solution.py:443
  120.7 5.6 %collective-permute-done.14 = f32[40,80]{1,0:T(8,128)S(1)} collective-permute-done((f32[40,80]{1,0:T(8,128)S(1)}, f32[40,80]{1,0:T(8,128)S(1)}, u32[]{:S(2)}, u32[]{:S(2)}) %collective-permute-start.14) | collective-permute-done | bytes 12832 | tf_op jit(solution)/shard_map/ppermute | solution.py:443
  127.1 3.0 %collective-permute-done.15 = f32[40,80]{1,0:T(8,128)S(1)} collective-permute-done((f32[40,80]{1,0:T(8,128)S(1)}, f32[40,80]{1,0:T(8,128)S(1)}, u32[]{:S(2)}, u32[]{:S(2)}) %collective-permute-start.15) | collective-permute-done | bytes 12832 | tf_op jit(solution)/shard_map/ppermute | solution.py:443
  130.3 4.8 %collective-permute-done.16 = f32[40,80]{1,0:T(8,128)S(1)} collective-permute-done((f32[40,80]{1,0:T(8,128)S(1)}, f32[40,80]{1,0:T(8,128)S(1)}, u32[]{:S(2)}, u32[]{:S(2)}) %collective-permute-start.16) | collective-permute-done | bytes 12832 | tf_op jit(solution)/shard_map/ppermute | solution.py:443
  136.2 3.4 %collective-permute-start.19 = (f32[40,80]{1,0:T(8,128)S(1)}, f32[40,80]{1,0:T(8,128)S(1)}, u32[]{:S(2)}, u32[]{:S(2)}) collective-permute-start(f32[40,80]{1,0:T(8,128)S(1)} %add.41), channel_id=1, source_target_pairs={{0,3},{1,2},{2,1},{3,0},{4,7},{5,6},{6,5},{7,4},{8,11},{9,10},{10,... | collective-permute-start | bytes 38408 | tf_op jit(solution)/shard_map/ppermute | solution.py:443
  140.0 1.6 %collective-permute-done.19 = f32[40,80]{1,0:T(8,128)S(1)} collective-permute-done((f32[40,80]{1,0:T(8,128)S(1)}, f32[40,80]{1,0:T(8,128)S(1)}, u32[]{:S(2)}, u32[]{:S(2)}) %collective-permute-start.19) | collective-permute-done | bytes 12832 | tf_op jit(solution)/shard_map/ppermute | solution.py:443
  (44 shorter events, 10.9 us)
Async XLA Ops:
  0.6 4.7 %copy-start = (f32[16,8,1024]{2,1,0:T(8,128)S(1)}, f32[16,8,1024]{2,1,0:T(8,128)}, u32[]{:S(2)}) copy-start(f32[16,8,1024]{2,1,0:T(8,128)} %refs_3_.1) | copy-start | bytes 1572868
  0.6 4.7 %copy-start.1 = (f32[8,8,1024]{2,1,0:T(8,128)S(1)}, f32[8,8,1024]{2,1,0:T(8,128)}, u32[]{:S(2)}) copy-start(f32[8,8,1024]{2,1,0:T(8,128)} %refs_4_.1) | copy-start | bytes 786436
  2.3 4.6 %collective-permute-start = (f32[25,8,128]{2,1,0:T(8,128)}, f32[25,8,128]{2,1,0:T(8,128)S(1)}, u32[]{:S(2)}, u32[]{:S(2)}) collective-permute-start(f32[25,8,128]{2,1,0:T(8,128)} %get-tuple-element.31), channel_id=1, source_target_pairs={{0,64},{64,128},{128,192},{1,65},{65,129},{129,193},{2,66},{66,130... | collective-permute-start | bytes 307208 | tf_op jit(solution)/shard_map/ppermute | solution.py:452
  4.1 6.2 %collective-permute-start.1 = (f32[25,8,128]{2,1,0:T(8,128)}, f32[25,8,128]{2,1,0:T(8,128)S(1)}, u32[]{:S(2)}, u32[]{:S(2)}) collective-permute-start(f32[25,8,128]{2,1,0:T(8,128)} %get-tuple-element.32), channel_id=1, source_target_pairs={{64,0},{128,64},{192,128},{65,1},{129,65},{193,129},{66,2},{130,66... | collective-permute-start | bytes 307208 | tf_op jit(solution)/shard_map/ppermute | solution.py:453
  11.7 10.0 %collective-permute-start.2 = (f32[25,8,640]{2,1,0:T(8,128)S(1)}, f32[25,8,640]{2,1,0:T(8,128)S(1)}, u32[]{:S(2)}, u32[]{:S(2)}) collective-permute-start(f32[25,8,640]{2,1,0:T(8,128)S(1)} %get-tuple-element.34), channel_id=1, source_target_pairs={{0,1},{1,0},{2,3},{3,2},{4,5},{5,4},{6,7},{7,6},{8,9},{9,8},{10,11... | collective-permute-start | bytes 1536008 | tf_op jit(solution)/shard_map/ppermute | solution.py:443
  21.7 47.4 %copy-start.4 = (f32[16]{0:T(128)S(1)}, f32[16]{0:T(128)}, u32[]{:S(2)}) copy-start(f32[16]{0:T(128)} %stiff_ref.1) | copy-start | bytes 196
  21.8 47.3 %copy-start.5 = (f32[16]{0:T(128)S(1)}, f32[16]{0:T(128)}, u32[]{:S(2)}) copy-start(f32[16]{0:T(128)} %dens_ref.1) | copy-start | bytes 196
  22.7 59.4 %collective-permute-start.3 = (f32[32,8,640]{2,1,0:T(8,128)}, f32[32,8,640]{2,1,0:T(8,128)S(1)}, u32[]{:S(2)}, u32[]{:S(2)}) collective-permute-start(f32[32,8,640]{2,1,0:T(8,128)} %pad_maximum_fusion), channel_id=1, source_target_pairs={{0,2},{1,3},{2,4},{3,5},{4,6},{5,7},{6,8},{7,9},{8,10},{9,11},{10,... | collective-permute-start | bytes 1966088 | tf_op jit(solution)/shard_map/ppermute | solution.py:428
  26.5 55.6 %collective-permute-start.4 = (f32[32,8,640]{2,1,0:T(8,128)}, f32[32,8,640]{2,1,0:T(8,128)S(1)}, u32[]{:S(2)}, u32[]{:S(2)}) collective-permute-start(f32[32,8,640]{2,1,0:T(8,128)} %pad_maximum_fusion), channel_id=1, source_target_pairs={{2,0},{3,1},{4,2},{5,3},{6,4},{7,5},{8,6},{9,7},{10,8},{11,9},{12,... | collective-permute-start | bytes 1966088 | tf_op jit(solution)/shard_map/ppermute | solution.py:428
  32.5 18.4 %collective-permute-start.5 = (f32[10,8,640]{2,1,0:T(8,128)S(1)}, f32[10,8,640]{2,1,0:T(8,128)S(1)}, u32[]{:S(2)}, u32[]{:S(2)}) collective-permute-start(f32[10,8,640]{2,1,0:T(8,128)S(1)} %get-tuple-element.35), channel_id=1, source_target_pairs={{1,5},{3,7},{4,0},{5,9},{6,2},{7,11},{8,4},{9,13},{10,6},{11,15},{... | collective-permute-start | bytes 614408 | tf_op jit(solution)/shard_map/ppermute | solution.py:434
  37.7 31.4 %collective-permute-start.7 = (f32[18,8,640]{2,1,0:T(8,128)}, f32[18,8,640]{2,1,0:T(8,128)S(1)}, u32[]{:S(2)}, u32[]{:S(2)}) collective-permute-start(f32[18,8,640]{2,1,0:T(8,128)} %pad_maximum_fusion.1), channel_id=1, source_target_pairs={{0,2},{1,3},{2,4},{3,5},{4,6},{5,7},{6,8},{7,9},{8,10},{9,11},{10,... | collective-permute-start | bytes 1105928 | tf_op jit(solution)/shard_map/ppermute | solution.py:428
  40.6 28.5 %collective-permute-start.8 = (f32[18,8,640]{2,1,0:T(8,128)}, f32[18,8,640]{2,1,0:T(8,128)S(1)}, u32[]{:S(2)}, u32[]{:S(2)}) collective-permute-start(f32[18,8,640]{2,1,0:T(8,128)} %pad_maximum_fusion.1), channel_id=1, source_target_pairs={{2,0},{3,1},{4,2},{5,3},{6,4},{7,5},{8,6},{9,7},{10,8},{11,9},{12,... | collective-permute-start | bytes 1105928 | tf_op jit(solution)/shard_map/ppermute | solution.py:428
  50.9 18.2 %collective-permute-start.6 = (f32[10,8,640]{2,1,0:T(8,128)}, f32[10,8,640]{2,1,0:T(8,128)S(1)}, u32[]{:S(2)}, u32[]{:S(2)}) collective-permute-start(f32[10,8,640]{2,1,0:T(8,128)} %get-tuple-element.36), channel_id=1, source_target_pairs={{1,4},{3,6},{4,1},{5,8},{6,3},{7,10},{8,5},{9,12},{10,7},{11,14},{... | collective-permute-start | bytes 614408 | tf_op jit(solution)/shard_map/ppermute | solution.py:434
  100.0 9.1 %collective-permute-start.10 = (f32[40,80]{1,0:T(8,128)S(1)}, f32[40,80]{1,0:T(8,128)S(1)}, u32[]{:S(2)}, u32[]{:S(2)}) collective-permute-start(f32[40,80]{1,0:T(8,128)S(1)} %get-tuple-element.50), channel_id=1, source_target_pairs={{0,128},{64,192},{128,0},{192,64},{1,129},{65,193},{129,1},{193,65... | collective-permute-start | bytes 38408 | tf_op jit(solution)/shard_map/ppermute | solution.py:480
  107.3 1.8 %collective-permute-start.11 = (f32[40,80]{1,0:T(8,128)S(1)}, f32[40,80]{1,0:T(8,128)S(1)}, u32[]{:S(2)}, u32[]{:S(2)}) collective-permute-start(f32[40,80]{1,0:T(8,128)S(1)} %get-tuple-element.51), channel_id=1, source_target_pairs={{0,192},{64,0},{128,64},{192,128},{1,193},{65,1},{129,65},{193,129... | collective-permute-start | bytes 38408 | tf_op jit(solution)/shard_map/ppermute | solution.py:480
  107.4 4.7 %collective-permute-start.9 = (f32[40,80]{1,0:T(8,128)S(1)}, f32[40,80]{1,0:T(8,128)S(1)}, u32[]{:S(2)}, u32[]{:S(2)}) collective-permute-start(f32[40,80]{1,0:T(8,128)S(1)} %get-tuple-element.49), channel_id=1, source_target_pairs={{0,64},{64,128},{128,192},{192,0},{1,65},{65,129},{129,193},{193,1... | collective-permute-start | bytes 38408 | tf_op jit(solution)/shard_map/ppermute | solution.py:480
  112.1 23.0 %collective-permute-start.12 = (f32[24,8,512]{2,1,0:T(8,128)S(1)}, f32[24,8,512]{2,1,0:T(8,128)S(1)}, u32[]{:S(2)}, u32[]{:S(2)}) collective-permute-start(f32[24,8,512]{2,1,0:T(8,128)S(1)} %get-tuple-element.52), channel_id=1, source_target_pairs={{0,1},{1,0},{2,3},{3,2},{4,5},{5,4},{6,7},{7,6},{8,9},{9,8},{10,11... | collective-permute-start | bytes 1179656 | tf_op jit(solution)/shard_map/ppermute | solution.py:443
  112.8 7.6 %collective-permute-start.13 = (f32[40,80]{1,0:T(8,128)S(1)}, f32[40,80]{1,0:T(8,128)S(1)}, u32[]{:S(2)}, u32[]{:S(2)}) collective-permute-start(f32[40,80]{1,0:T(8,128)S(1)} %add_add_fusion.1), channel_id=1, source_target_pairs={{0,4},{1,5},{2,6},{3,7},{4,0},{5,1},{6,2},{7,3},{8,12},{9,13},{10,... | collective-permute-start | bytes 38408 | tf_op jit(solution)/shard_map/ppermute | solution.py:443
  120.4 5.9 %collective-permute-start.14 = (f32[40,80]{1,0:T(8,128)S(1)}, f32[40,80]{1,0:T(8,128)S(1)}, u32[]{:S(2)}, u32[]{:S(2)}) collective-permute-start(f32[40,80]{1,0:T(8,128)S(1)} %add.38), channel_id=1, source_target_pairs={{0,12},{1,13},{2,14},{3,15},{4,8},{5,9},{6,10},{7,11},{8,4},{9,5},... | collective-permute-start | bytes 38408 | tf_op jit(solution)/shard_map/ppermute | solution.py:443
  126.3 3.8 %collective-permute-start.15 = (f32[40,80]{1,0:T(8,128)S(1)}, f32[40,80]{1,0:T(8,128)S(1)}, u32[]{:S(2)}, u32[]{:S(2)}) collective-permute-start(f32[40,80]{1,0:T(8,128)S(1)} %add.39), channel_id=1, source_target_pairs={{0,16},{1,17},{2,18},{3,19},{4,20},{5,21},{6,22},{7,23},{8,24},{9,... | collective-permute-start | bytes 38408 | tf_op jit(solution)/shard_map/ppermute | solution.py:443
  130.1 5.0 %collective-permute-start.16 = (f32[40,80]{1,0:T(8,128)S(1)}, f32[40,80]{1,0:T(8,128)S(1)}, u32[]{:S(2)}, u32[]{:S(2)}) collective-permute-start(f32[40,80]{1,0:T(8,128)S(1)} %add.40), channel_id=1, source_target_pairs={{0,48},{1,49},{2,50},{3,51},{4,52},{5,53},{6,54},{7,55},{8,56},{9,... | collective-permute-start | bytes 38408 | tf_op jit(solution)/shard_map/ppermute | solution.py:443
  136.1 3.8 %collective-permute-start.17 = (f32[40,80]{1,0:T(8,128)S(1)}, f32[40,80]{1,0:T(8,128)S(1)}, u32[]{:S(2)}, u32[]{:S(2)}) collective-permute-start(f32[40,80]{1,0:T(8,128)S(1)} %add.41), channel_id=1, source_target_pairs={{0,1},{1,0},{2,3},{3,2},{4,5},{5,4},{6,7},{7,6},{8,9},{9,8},{10,11... | collective-permute-start | bytes 38408 | tf_op jit(solution)/shard_map/ppermute | solution.py:443
  136.2 3.8 %collective-permute-start.18 = (f32[40,80]{1,0:T(8,128)S(1)}, f32[40,80]{1,0:T(8,128)S(1)}, u32[]{:S(2)}, u32[]{:S(2)}) collective-permute-start(f32[40,80]{1,0:T(8,128)S(1)} %add.41), channel_id=1, source_target_pairs={{0,2},{1,3},{2,0},{3,1},{4,6},{5,7},{6,4},{7,5},{8,10},{9,11},{10,... | collective-permute-start | bytes 38408 | tf_op jit(solution)/shard_map/ppermute | solution.py:443
  136.2 5.4 %collective-permute-start.19 = (f32[40,80]{1,0:T(8,128)S(1)}, f32[40,80]{1,0:T(8,128)S(1)}, u32[]{:S(2)}, u32[]{:S(2)}) collective-permute-start(f32[40,80]{1,0:T(8,128)S(1)} %add.41), channel_id=1, source_target_pairs={{0,3},{1,2},{2,1},{3,0},{4,7},{5,6},{6,5},{7,4},{8,11},{9,10},{10,... | collective-permute-start | bytes 38408 | tf_op jit(solution)/shard_map/ppermute | solution.py:443
  (2 other events, 9.5 us)

commit v2 on v1

--- a/solution.py
+++ b/solution.py
@@ -34,6 +34,7 @@
 SENS_SLABS = ROWS + 1
 ACT_SLABS = ROWS * ACT_SETS
 ALL_ROWS = 64
+ROOM = 80
 DT = 0.35
 
 
@@ -139,11 +140,11 @@
     low_side = side_ref[0] == 0
     (fields_0, ids_0), (fields_1, ids_1) = blocks
     near = NEAR * SETS
-    keep_s_ref, keep_a_ref, give_ref, far_keep_ref, far_give_ref = out_refs
+    keep_s_ref, keep_a_ref, far_keep_ref, give_s_ref, give_a_ref, far_give_ref = out_refs
     for sens_ref, act_ref, far_ref, fields, ids in (
         (keep_s_ref, keep_a_ref, far_keep_ref, jnp.where(low_side, fields_0, fields_1), jnp.where(low_side, ids_0, ids_1)),
         (
-            give_ref.at[0:SENS_SLABS], give_ref.at[SENS_SLABS:], far_give_ref,
+            give_s_ref, give_a_ref, far_give_ref,
             jnp.where(low_side, fields_1, fields_0), jnp.where(low_side, ids_1, ids_0),
         ),
     ):
@@ -261,7 +262,7 @@
     p_ref, u_ref, s_ref, m_ref, fs_ref,
 ):
     side = side_ref[0]
-    strips = [keep_ref, give_ref.at[0:SENS_SLABS]]
+    strips = [keep_ref, give_ref]
     for ref in (up_ref, dn_ref):
         strips += [ref.at[0:SENS_SLABS], ref.at[SENS_SLABS:]]
     far = (far_keep_ref, far_give_ref)
@@ -310,7 +311,7 @@
         fs_ref[at, rows, 0:WIDE] = p_ref[spot] * mask
         fs_ref[at, rows, WIDE : 2 * WIDE] = u_ref[spot] * fast
 
-    march(1, 8, keep_row, mask_ref, p_ref, u_ref, fx_ref, fy_ref, fw_ref, mk_ref)
+    march(1, 16, keep_row, mask_ref, p_ref, u_ref, fx_ref, fy_ref, fw_ref, mk_ref)
 
     def narrow(row, carry):
         frames_ref[row] = fs_ref[row].astype(jnp.bfloat16)
@@ -329,7 +330,7 @@
     p_ref, u_ref, fa_ref, acc_ref,
 ):
     side = side_ref[0]
-    strips = [keep_ref, give_ref.at[SENS_SLABS:]]
+    strips = [keep_ref, give_ref]
     for ref in (up_ref, dn_ref):
         strips += [ref.at[0:ACT_SLABS], ref.at[ACT_SLABS:]]
     fill(side, strips, (far_keep_ref, far_give_ref), ACT_SETS, 0, p_ref, u_ref, mk_ref)
@@ -391,17 +392,28 @@
     )(*scalars, *operands)
 
 
+def join_kernel(first_ref, second_ref, out_ref):
+    count = first_ref.shape[0]
+    out_ref[0:count] = first_ref[...]
+    out_ref[count:] = second_ref[...]
+
+
+def joined(first, second):
+    count = first.shape[0]
+    return call(join_kernel, (), (first, second), (array(2 * count, 8, WIDE),), [], 8)[0]
+
+
 def sensor_block(scalars, operands):
-    face = array(ALL_ROWS, 8, WIDE)
+    face = array(ROOM, 8, WIDE)
     part = array(SENS, ROWS, HALF)
     return call(
         sensor_kernel, scalars, operands,
         (
             part, part, array(CENTRE_ROWS, SENS * SNAPS, 2 * WIDE, dtype=jnp.bfloat16),
-            face, face, array(ALL_ROWS, 8, LANES), face, array(2, LANES - FLAG_LANE, WIDE),
+            face, face, array(ROOM, 8, LANES), face, array(2, LANES - FLAG_LANE, WIDE),
         ),
         [
-            scratch(ALL_ROWS, 8, WIDE), scratch(ALL_ROWS, 8, WIDE), scratch(ALL_ROWS, WIDE), scratch(ALL_ROWS, WIDE),
+            scratch(ROOM, 8, WIDE), scratch(ROOM, 8, WIDE), scratch(ALL_ROWS, WIDE), scratch(ALL_ROWS, WIDE),
             scratch(CENTRE_ROWS, SENS * SNAPS, 2 * WIDE),
         ],
         28,
@@ -410,7 +422,7 @@
 
 def actuator_block(scalars, operands):
     part = array(RESP, ROWS, HALF)
-    state = scratch(ALL_ROWS * ACT_SETS, 8, WIDE)
+    state = scratch(ROOM * ACT_SETS, 8, WIDE)
     return call(
         actuator_kernel, scalars, operands,
         (part, part) + (array(SHARE, SENS * SNAPS),) * 4,
@@ -460,32 +472,32 @@
         main_kernel, out_shape=(block, block), in_specs=[vmem] * 4, out_specs=(vmem, vmem), compiler_params=grant(16)
     )(actuator_fields, sensor_fields, region_ids, flags)
     far = array(FAR, 8, WIDE)
-    outs = (array(SENS_SLABS, 8, WIDE), array(ACT_SLABS, 8, WIDE), block, far, far)
-    keep_s, keep_a, give, far_keep, far_give = call(halo_kernel, (side_word,), (first, second, left, right), outs, [], 16)
-
+    outs = (array(SENS_SLABS, 8, WIDE), array(ACT_SLABS, 8, WIDE), far)
+    keep_s, keep_a, far_keep, give_s, give_a, far_give = call(
+        halo_kernel, (side_word,), (first, second, left, right), outs + outs, [], 16
+    )
+
+    got_s = swap(give_s, 1)
+    got_a = swap(give_a, 1)
     far_keep = outward(far_keep, 4)
-    got = swap(give, 1)
     far_give = outward(far_give, 3)
-    both_s = jnp.concatenate([keep_s, got[:SENS_SLABS]], 0)
+    both_s = joined(keep_s, got_s)
     up_s = along_dom(both_s, 2)
     dn_s = along_dom(both_s, -2)
-    both_a = jnp.concatenate([keep_a, got[SENS_SLABS:]], 0)
+    both_a = joined(keep_a, got_a)
     up_a = along_dom(both_a, 2)
     dn_a = along_dom(both_a, -2)
     far = (far_keep, far_give)
-    sensor = sensor_block((side_word, stiffness_table, density_table), (keep_s, got, up_s, dn_s) + far)
-    own, other, *pieces = actuator_block((side_word, place_word), (keep_a, got, up_a, dn_a) + far + tuple(sensor))
+    sensor = sensor_block((side_word, stiffness_table, density_table), (keep_s, got_s, up_s, dn_s) + far)
+    own, other, *pieces = actuator_block((side_word, place_word), (keep_a, got_a, up_a, dn_a) + far + tuple(sensor))
     total = pieces[0]
     for hop in range(1, sections):
         total = total + lax.ppermute(pieces[hop], "sec", [(i, (i + hop) % sections) for i in range(sections)])
     other, total = lax.optimization_barrier((other, total))
     back = swap(other, 1)
-    position = jnp.where(
-        side == 0, jnp.concatenate([own, back], 2), jnp.concatenate([back, own], 2)
-    )
     for bits in (4, 12, 16, 48):
         total = total + swap(total, bits)
-    position, total = lax.optimization_barrier((position, total))
+    position = jnp.where(side == 0, jnp.concatenate([own, back], 2), jnp.concatenate([back, own], 2))
     total = total + sum(swap(total, bits) for bits in (1, 2, 3))
     return (position, total)
 

time: 142 us -> 137 us (0.965)
  waiting for transfers between devices: 55.8 us -> 49 us
  other arithmetic: 3.25 us -> 1.6 us
    ppermute x3, waiting for transfers between devices: 4.36 us -> 1.48 us  [body(): lax.ppermute(pieces[hop], 'sec', [(i, (i + hop) % sections) for i in rang...]
    ppermute x9 -> x10, waiting for transfers between devices: 26.6 us -> 24.2 us  [swap(): return lax.ppermute(cells, 'dom', [(i, i ^ bit) for i in range(count)])]
    ppermute x3, starting transfers between devices: 7.73 us -> 9.97 us  [body(): lax.ppermute(pieces[hop], 'sec', [(i, (i + hop) % sections) for i in rang...]
    concatenate x2 -> x0, other arithmetic: 1.65 us -> none  [the longest x1 0.88 us: body(): both_a = jnp.concatenate([keep_a, got[SENS_SLABS:]], 0)]
    ppermute x2, waiting for transfers between devices: 21.5 us -> 19.9 us  [outward(): lax.ppermute(cells, 'dom', [(i, j) for i, j in pairs if 0 <= j < count])]
    pallas_call x3 -> x5, Pallas kernels: 32.3 us -> 33.6 us  [call(): pl.pallas_call(kernel, out_shape=out_shape, in_specs=[smem] * len(scalars...]
    ppermute x9 -> x10, starting transfers between devices: 11.8 us -> 10.9 us  [swap(): return lax.ppermute(cells, 'dom', [(i, i ^ bit) for i in range(count)])]
  transfers between devices with their start and end apart: 20 -> 21, of which waited for: 13 -> 13; matrix products, arithmetic and copies ran while one was open for 1% -> 0% of each run, Pallas kernels for 10% -> 11%
where the time goes in v2:
time: 137 us; the launch traced here: 136 us
  waiting for transfers between devices  49 us (36%)
  starting transfers between devices  48.1 us (35%)
  Pallas kernels  36.7 us (27%)
  other arithmetic  1.6 us (1%)
    pallas_call x5, Pallas kernels, call(): pl.pallas_call(kernel, out_shape=out_shape, in_specs=[smem] * len(scalars...  33.6 us
    ppermute x10, waiting for transfers between devices, swap(): return lax.ppermute(cells, 'dom', [(i, i ^ bit) for i in range(count)])  24.2 us
    ppermute x2, waiting for transfers between devices, outward(): lax.ppermute(cells, 'dom', [(i, j) for i, j in pairs if 0 <= j < count])  19.9 us
    ppermute x4, starting transfers between devices, along_dom(): lax.ppermute(cells, 'dom', [(i, i + distance) for i in range(count) if 0...  17.8 us
    ppermute x10, starting transfers between devices, swap(): return lax.ppermute(cells, 'dom', [(i, i ^ bit) for i in range(count)])  10.9 us
    ppermute x3, starting transfers between devices, body(): lax.ppermute(pieces[hop], 'sec', [(i, (i + hop) % sections) for i in rang...  9.97 us
    ppermute x2, starting transfers between devices, outward(): lax.ppermute(cells, 'dom', [(i, j) for i, j in pairs if 0 <= j < count])  6.45 us
    ppermute x1, waiting for transfers between devices, body(): lax.ppermute(left_edge, 'sec', [(i + 1, i) for i in range(sections - 1)])  3.36 us
  transfers between devices with their start and end apart: 21, of which 13 were waited for; matrix products, arithmetic and copies ran while one was open for 0% of the time, Pallas kernels for 11%

profile of v2, /device:TPU:24, one launch (start us, length us, event | category | flops | bytes accessed | tf_op | source)
XLA Modules:
  0.0 136.3 jit_solution(10081146763775992485)
XLA Ops:
  0.7 1.6 %shard_map.78 = (f32[25,8,128]{2,1,0:T(8,128)}, f32[25,8,128]{2,1,0:T(8,128)}) custom-call(f32[16,8,1024]{2,1,0:T(8,128)} %refs_3_.1, f32[8,8,1024]{2,1,0:T(8,128)} %refs_4_.1, s32[8,1024]{1,0:T(8,128)} %refs_5_.1, f32[16,8,1024]{2,1,0:T(8,128)} %refs_3_.1, f32[8,8,1024]{2,1,0:T(8,128)} %refs_4_.1, s32[8,1024]{1,0:T(8,128)} %refs_5_.1), custom_call_target="tpu_custom_call" | custom-call | tf_op jit(solution)/shard_map/pallas_call | solution.py:93
  2.3 1.7 %collective-permute-start = (f32[25,8,128]{2,1,0:T(8,128)}, f32[25,8,128]{2,1,0:T(8,128)S(1)}, u32[]{:S(2)}, u32[]{:S(2)}) collective-permute-start(f32[25,8,128]{2,1,0:T(8,128)} %get-tuple-element.30), channel_id=1, source_target_pairs={{0,64},{64,128},{128,192},{1,65},{65,129},{129,193},{2,66},{66,130... | collective-permute-start | bytes 307208 | tf_op jit(solution)/shard_map/ppermute | solution.py:464
  5.4 1.5 %shard_map.77 = (f32[25,8,640]{2,1,0:T(8,128)S(1)}, f32[25,8,640]{2,1,0:T(8,128)S(1)}) custom-call(f32[16,8,1024]{2,1,0:T(8,128)S(1)} %copy-done, f32[8,8,1024]{2,1,0:T(8,128)S(1)} %copy-done.1, s32[8,1024]{1,0:T(8,128)S(1)} %copy-done.2, s32[8,10]{1,0:T(8,128)S(1)} %bitcast.5), custom_call_target="tpu_custom_call" | custom-call | tf_op jit(solution)/shard_map/pallas_call | solution.py:471
  6.9 3.4 %collective-permute-done.1.right_ref = f32[25,8,128]{2,1,0:T(8,128)S(1)} collective-permute-done((f32[25,8,128]{2,1,0:T(8,128)}, f32[25,8,128]{2,1,0:T(8,128)S(1)}, u32[]{:S(2)}, u32[]{:S(2)}) %collective-permute-start.1) | collective-permute-done | bytes 102432 | tf_op jit(solution)/shard_map/ppermute | solution.py:465
  12.3 6.5 %collective-permute-done.2.second_ref.give_ref = f32[16,8,640]{2,1,0:T(8,128)S(1)} collective-permute-done((f32[16,8,640]{2,1,0:T(8,128)S(1)}, f32[16,8,640]{2,1,0:T(8,128)S(1)}, u32[]{:S(2)}, u32[]{:S(2)}) %collective-permute-start.2) | collective-permute-done | bytes 327712 | tf_op jit(solution)/shard_map/ppermute | solution.py:455
  18.9 3.8 %collective-permute-start.3 = (f32[32,8,640]{2,1,0:T(8,128)S(1)}, f32[32,8,640]{2,1,0:T(8,128)S(1)}, u32[]{:S(2)}, u32[]{:S(2)}) collective-permute-start(f32[32,8,640]{2,1,0:T(8,128)S(1)} %shard_map.80), channel_id=1, source_target_pairs={{0,2},{1,3},{2,4},{3,5},{4,6},{5,7},{6,8},{7,9},{8,10},{9,11},{10,... | collective-permute-start | bytes 1966088 | tf_op jit(solution)/shard_map/ppermute | solution.py:440
  22.7 6.0 %collective-permute-start.4 = (f32[32,8,640]{2,1,0:T(8,128)S(1)}, f32[32,8,640]{2,1,0:T(8,128)S(1)}, u32[]{:S(2)}, u32[]{:S(2)}) collective-permute-start(f32[32,8,640]{2,1,0:T(8,128)S(1)} %shard_map.80), channel_id=1, source_target_pairs={{2,0},{3,1},{4,2},{5,3},{6,4},{7,5},{8,6},{9,7},{10,8},{11,9},{12,... | collective-permute-start | bytes 1966088 | tf_op jit(solution)/shard_map/ppermute | solution.py:440
  29.4 4.3 %collective-permute-start.5 = (f32[10,8,640]{2,1,0:T(8,128)S(1)}, f32[10,8,640]{2,1,0:T(8,128)S(1)}, u32[]{:S(2)}, u32[]{:S(2)}) collective-permute-start(f32[10,8,640]{2,1,0:T(8,128)S(1)} %get-tuple-element.34), channel_id=1, source_target_pairs={{1,5},{3,7},{4,0},{5,9},{6,2},{7,11},{8,4},{9,13},{10,6},{11,15},{... | collective-permute-start | bytes 614408 | tf_op jit(solution)/shard_map/ppermute | solution.py:446
  35.1 2.3 %collective-permute-start.8 = (f32[18,8,640]{2,1,0:T(8,128)}, f32[18,8,640]{2,1,0:T(8,128)}, u32[]{:S(2)}, u32[]{:S(2)}) collective-permute-start(f32[18,8,640]{2,1,0:T(8,128)} %shard_map.81), channel_id=1, source_target_pairs={{0,2},{1,3},{2,4},{3,5},{4,6},{5,7},{6,8},{7,9},{8,10},{9,11},{10,... | collective-permute-start | bytes 1105928 | tf_op jit(solution)/shard_map/ppermute | solution.py:440
  37.5 5.6 %collective-permute-start.9 = (f32[18,8,640]{2,1,0:T(8,128)}, f32[18,8,640]{2,1,0:T(8,128)}, u32[]{:S(2)}, u32[]{:S(2)}) collective-permute-start(f32[18,8,640]{2,1,0:T(8,128)} %shard_map.81), channel_id=1, source_target_pairs={{2,0},{3,1},{4,2},{5,3},{6,4},{7,5},{8,6},{9,7},{10,8},{11,9},{12,... | collective-permute-start | bytes 1105928 | tf_op jit(solution)/shard_map/ppermute | solution.py:440
  43.1 3.9 %collective-permute-done.5.far_keep_ref = f32[10,8,640]{2,1,0:T(8,128)S(1)} collective-permute-done((f32[10,8,640]{2,1,0:T(8,128)S(1)}, f32[10,8,640]{2,1,0:T(8,128)S(1)}, u32[]{:S(2)}, u32[]{:S(2)}) %collective-permute-start.5) | collective-permute-done | bytes 204832 | tf_op jit(solution)/shard_map/ppermute | solution.py:446
  47.0 2.1 %collective-permute-start.6 = (f32[10,8,640]{2,1,0:T(8,128)}, f32[10,8,640]{2,1,0:T(8,128)S(1)}, u32[]{:S(2)}, u32[]{:S(2)}) collective-permute-start(f32[10,8,640]{2,1,0:T(8,128)} %get-tuple-element.35), channel_id=1, source_target_pairs={{1,4},{3,6},{4,1},{5,8},{6,3},{7,10},{8,5},{9,12},{10,7},{11,14},{... | collective-permute-start | bytes 614408 | tf_op jit(solution)/shard_map/ppermute | solution.py:446
  49.1 16.0 %collective-permute-done.6.far_give_ref = f32[10,8,640]{2,1,0:T(8,128)S(1)} collective-permute-done((f32[10,8,640]{2,1,0:T(8,128)}, f32[10,8,640]{2,1,0:T(8,128)S(1)}, u32[]{:S(2)}, u32[]{:S(2)}) %collective-permute-start.6) | collective-permute-done | bytes 204832 | tf_op jit(solution)/shard_map/ppermute | solution.py:446
  65.2 12.6 %shard_map.82 = (f32[8,8,512]{2,1,0:T(8,128)S(1)}, f32[8,8,512]{2,1,0:T(8,128)S(1)}, bf16[16,80,1280]{2,1,0:T(8,128)(2,1)S(1)}, f32[80,8,640]{2,1,0:T(8,128)S(1)...) custom-call(s32[1]{0:T(128)} %bitcast.side_ref, ...), custom_call_target="tpu_custom_call" | custom-call | tf_op jit(solution)/shard_map/pallas_call | solution.py:385
  77.8 18.7 %shard_map.83 = (f32[24,8,512]{2,1,0:T(8,128)S(1)}, f32[24,8,512]{2,1,0:T(8,128)S(1)}, f32[40,80]{1,0:T(8,128)S(1)}, f32[40,80]{1,0:T(8,128)S(1)}, f32[40,80]{1,0:T(8,128)S(1)}, /*index=5*/f32[40,80]{1,0:T(8,128)S(1)}) custom-call(s32[1]{0:T(128)} %bitcast.side_ref, s32[1]{0:T(128)} %bitcast.1.place_ref, ...), custom_call_target="tpu_custom_call" | custom-call | tf_op jit(solution)/shard_map/pallas_call | solution.py:385
  96.5 4.5 %collective-permute-start.10 = (f32[40,80]{1,0:T(8,128)S(1)}, f32[40,80]{1,0:T(8,128)S(1)}, u32[]{:S(2)}, u32[]{:S(2)}) collective-permute-start(f32[40,80]{1,0:T(8,128)S(1)} %get-tuple-element.49), channel_id=1, source_target_pairs={{0,64},{64,128},{128,192},{192,0},{1,65},{65,129},{129,193},{193,1... | collective-permute-start | bytes 38408 | tf_op jit(solution)/shard_map/ppermute | solution.py:495
  100.9 2.6 %collective-permute-start.11 = (f32[40,80]{1,0:T(8,128)S(1)}, f32[40,80]{1,0:T(8,128)S(1)}, u32[]{:S(2)}, u32[]{:S(2)}) collective-permute-start(f32[40,80]{1,0:T(8,128)S(1)} %get-tuple-element.50), channel_id=1, source_target_pairs={{0,128},{64,192},{128,0},{192,64},{1,129},{65,193},{129,1},{193,65... | collective-permute-start | bytes 38408 | tf_op jit(solution)/shard_map/ppermute | solution.py:495
  103.6 2.9 %collective-permute-start.12 = (f32[40,80]{1,0:T(8,128)S(1)}, f32[40,80]{1,0:T(8,128)S(1)}, u32[]{:S(2)}, u32[]{:S(2)}) collective-permute-start(f32[40,80]{1,0:T(8,128)S(1)} %get-tuple-element.51), channel_id=1, source_target_pairs={{0,192},{64,0},{128,64},{192,128},{1,193},{65,1},{129,65},{193,129... | collective-permute-start | bytes 38408 | tf_op jit(solution)/shard_map/ppermute | solution.py:495
  108.2 4.6 %collective-permute-start.14 = (f32[40,80]{1,0:T(8,128)S(1)}, f32[40,80]{1,0:T(8,128)S(1)}, u32[]{:S(2)}, u32[]{:S(2)}) collective-permute-start(f32[40,80]{1,0:T(8,128)S(1)} %add_add_fusion.1), channel_id=1, source_target_pairs={{0,4},{1,5},{2,6},{3,7},{4,0},{5,1},{6,2},{7,3},{8,12},{9,13},{10,... | collective-permute-start | bytes 38408 | tf_op jit(solution)/shard_map/ppermute | solution.py:455
  112.8 1.8 %collective-permute-done.14 = f32[40,80]{1,0:T(8,128)S(1)} collective-permute-done((f32[40,80]{1,0:T(8,128)S(1)}, f32[40,80]{1,0:T(8,128)S(1)}, u32[]{:S(2)}, u32[]{:S(2)}) %collective-permute-start.14) | collective-permute-done | bytes 12832 | tf_op jit(solution)/shard_map/ppermute | solution.py:455
  114.8 5.6 %collective-permute-done.15 = f32[40,80]{1,0:T(8,128)S(1)} collective-permute-done((f32[40,80]{1,0:T(8,128)S(1)}, f32[40,80]{1,0:T(8,128)S(1)}, u32[]{:S(2)}, u32[]{:S(2)}) %collective-permute-start.15) | collective-permute-done | bytes 12832 | tf_op jit(solution)/shard_map/ppermute | solution.py:455
  121.2 3.0 %collective-permute-done.16 = f32[40,80]{1,0:T(8,128)S(1)} collective-permute-done((f32[40,80]{1,0:T(8,128)S(1)}, f32[40,80]{1,0:T(8,128)S(1)}, u32[]{:S(2)}, u32[]{:S(2)}) %collective-permute-start.16) | collective-permute-done | bytes 12832 | tf_op jit(solution)/shard_map/ppermute | solution.py:455
  124.5 4.7 %collective-permute-done.17 = f32[40,80]{1,0:T(8,128)S(1)} collective-permute-done((f32[40,80]{1,0:T(8,128)S(1)}, f32[40,80]{1,0:T(8,128)S(1)}, u32[]{:S(2)}, u32[]{:S(2)}) %collective-permute-start.17) | collective-permute-done | bytes 12832 | tf_op jit(solution)/shard_map/ppermute | solution.py:455
  129.5 3.2 %collective-permute-start.20 = (f32[40,80]{1,0:T(8,128)S(1)}, f32[40,80]{1,0:T(8,128)S(1)}, u32[]{:S(2)}, u32[]{:S(2)}) collective-permute-start(f32[40,80]{1,0:T(8,128)S(1)} %add.41), channel_id=1, source_target_pairs={{0,3},{1,2},{2,1},{3,0},{4,7},{5,6},{6,5},{7,4},{8,11},{9,10},{10,... | collective-permute-start | bytes 38408 | tf_op jit(solution)/shard_map/ppermute | solution.py:455
  (44 shorter events, 12.4 us)
Async XLA Ops:
  0.6 4.7 %copy-start = (f32[16,8,1024]{2,1,0:T(8,128)S(1)}, f32[16,8,1024]{2,1,0:T(8,128)}, u32[]{:S(2)}) copy-start(f32[16,8,1024]{2,1,0:T(8,128)} %refs_3_.1) | copy-start | bytes 1572868
  2.3 4.6 %collective-permute-start = (f32[25,8,128]{2,1,0:T(8,128)}, f32[25,8,128]{2,1,0:T(8,128)S(1)}, u32[]{:S(2)}, u32[]{:S(2)}) collective-permute-start(f32[25,8,128]{2,1,0:T(8,128)} %get-tuple-element.30), channel_id=1, source_target_pairs={{0,64},{64,128},{128,192},{1,65},{65,129},{129,193},{2,66},{66,130... | collective-permute-start | bytes 307208 | tf_op jit(solution)/shard_map/ppermute | solution.py:464
  4.1 6.2 %collective-permute-start.1 = (f32[25,8,128]{2,1,0:T(8,128)}, f32[25,8,128]{2,1,0:T(8,128)S(1)}, u32[]{:S(2)}, u32[]{:S(2)}) collective-permute-start(f32[25,8,128]{2,1,0:T(8,128)} %get-tuple-element.31), channel_id=1, source_target_pairs={{64,0},{128,64},{192,128},{65,1},{129,65},{193,129},{66,2},{130,66... | collective-permute-start | bytes 307208 | tf_op jit(solution)/shard_map/ppermute | solution.py:465
  10.3 54.9 %copy-start.4 = (f32[16]{0:T(128)S(1)}, f32[16]{0:T(128)}, u32[]{:S(2)}) copy-start(f32[16]{0:T(128)} %stiff_ref.1) | copy-start | bytes 196
  10.3 54.9 %copy-start.5 = (f32[16]{0:T(128)S(1)}, f32[16]{0:T(128)}, u32[]{:S(2)}) copy-start(f32[16]{0:T(128)} %dens_ref.1) | copy-start | bytes 196
  11.8 7.1 %collective-permute-start.2 = (f32[16,8,640]{2,1,0:T(8,128)S(1)}, f32[16,8,640]{2,1,0:T(8,128)S(1)}, u32[]{:S(2)}, u32[]{:S(2)}) collective-permute-start(f32[16,8,640]{2,1,0:T(8,128)S(1)} %get-tuple-element.33), channel_id=1, source_target_pairs={{0,1},{1,0},{2,3},{3,2},{4,5},{5,4},{6,7},{7,6},{8,9},{9,8},{10,11... | collective-permute-start | bytes 983048 | tf_op jit(solution)/shard_map/ppermute | solution.py:455
  18.9 58.9 %collective-permute-start.3 = (f32[32,8,640]{2,1,0:T(8,128)S(1)}, f32[32,8,640]{2,1,0:T(8,128)S(1)}, u32[]{:S(2)}, u32[]{:S(2)}) collective-permute-start(f32[32,8,640]{2,1,0:T(8,128)S(1)} %shard_map.80), channel_id=1, source_target_pairs={{0,2},{1,3},{2,4},{3,5},{4,6},{5,7},{6,8},{7,9},{8,10},{9,11},{10,... | collective-permute-start | bytes 1966088 | tf_op jit(solution)/shard_map/ppermute | solution.py:440
  22.7 55.1 %collective-permute-start.4 = (f32[32,8,640]{2,1,0:T(8,128)S(1)}, f32[32,8,640]{2,1,0:T(8,128)S(1)}, u32[]{:S(2)}, u32[]{:S(2)}) collective-permute-start(f32[32,8,640]{2,1,0:T(8,128)S(1)} %shard_map.80), channel_id=1, source_target_pairs={{2,0},{3,1},{4,2},{5,3},{6,4},{7,5},{8,6},{9,7},{10,8},{11,9},{12,... | collective-permute-start | bytes 1966088 | tf_op jit(solution)/shard_map/ppermute | solution.py:440
  28.8 5.6 %collective-permute-start.7 = (f32[9,8,640]{2,1,0:T(8,128)S(1)}, f32[9,8,640]{2,1,0:T(8,128)S(1)}, u32[]{:S(2)}, u32[]{:S(2)}) collective-permute-start(f32[9,8,640]{2,1,0:T(8,128)S(1)} %get-tuple-element.37), channel_id=1, source_target_pairs={{0,1},{1,0},{2,3},{3,2},{4,5},{5,4},{6,7},{7,6},{8,9},{9,8},{10,11... | collective-permute-start | bytes 552968 | tf_op jit(solution)/shard_map/ppermute | solution.py:455
  29.4 17.6 %collective-permute-start.5 = (f32[10,8,640]{2,1,0:T(8,128)S(1)}, f32[10,8,640]{2,1,0:T(8,128)S(1)}, u32[]{:S(2)}, u32[]{:S(2)}) collective-permute-start(f32[10,8,640]{2,1,0:T(8,128)S(1)} %get-tuple-element.34), channel_id=1, source_target_pairs={{1,5},{3,7},{4,0},{5,9},{6,2},{7,11},{8,4},{9,13},{10,6},{11,15},{... | collective-permute-start | bytes 614408 | tf_op jit(solution)/shard_map/ppermute | solution.py:446
  35.1 30.0 %collective-permute-start.8 = (f32[18,8,640]{2,1,0:T(8,128)}, f32[18,8,640]{2,1,0:T(8,128)}, u32[]{:S(2)}, u32[]{:S(2)}) collective-permute-start(f32[18,8,640]{2,1,0:T(8,128)} %shard_map.81), channel_id=1, source_target_pairs={{0,2},{1,3},{2,4},{3,5},{4,6},{5,7},{6,8},{7,9},{8,10},{9,11},{10,... | collective-permute-start | bytes 1105928 | tf_op jit(solution)/shard_map/ppermute | solution.py:440
  37.5 27.6 %collective-permute-start.9 = (f32[18,8,640]{2,1,0:T(8,128)}, f32[18,8,640]{2,1,0:T(8,128)}, u32[]{:S(2)}, u32[]{:S(2)}) collective-permute-start(f32[18,8,640]{2,1,0:T(8,128)} %shard_map.81), channel_id=1, source_target_pairs={{2,0},{3,1},{4,2},{5,3},{6,4},{7,5},{8,6},{9,7},{10,8},{11,9},{12,... | collective-permute-start | bytes 1105928 | tf_op jit(solution)/shard_map/ppermute | solution.py:440
  47.0 18.1 %collective-permute-start.6 = (f32[10,8,640]{2,1,0:T(8,128)}, f32[10,8,640]{2,1,0:T(8,128)S(1)}, u32[]{:S(2)}, u32[]{:S(2)}) collective-permute-start(f32[10,8,640]{2,1,0:T(8,128)} %get-tuple-element.35), channel_id=1, source_target_pairs={{1,4},{3,6},{4,1},{5,8},{6,3},{7,10},{8,5},{9,12},{10,7},{11,14},{... | collective-permute-start | bytes 614408 | tf_op jit(solution)/shard_map/ppermute | solution.py:446
  96.5 10.0 %collective-permute-start.10 = (f32[40,80]{1,0:T(8,128)S(1)}, f32[40,80]{1,0:T(8,128)S(1)}, u32[]{:S(2)}, u32[]{:S(2)}) collective-permute-start(f32[40,80]{1,0:T(8,128)S(1)} %get-tuple-element.49), channel_id=1, source_target_pairs={{0,64},{64,128},{128,192},{192,0},{1,65},{65,129},{129,193},{193,1... | collective-permute-start | bytes 38408 | tf_op jit(solution)/shard_map/ppermute | solution.py:495
  100.9 5.5 %collective-permute-start.11 = (f32[40,80]{1,0:T(8,128)S(1)}, f32[40,80]{1,0:T(8,128)S(1)}, u32[]{:S(2)}, u32[]{:S(2)}) collective-permute-start(f32[40,80]{1,0:T(8,128)S(1)} %get-tuple-element.50), channel_id=1, source_target_pairs={{0,128},{64,192},{128,0},{192,64},{1,129},{65,193},{129,1},{193,65... | collective-permute-start | bytes 38408 | tf_op jit(solution)/shard_map/ppermute | solution.py:495
  103.6 4.4 %collective-permute-start.12 = (f32[40,80]{1,0:T(8,128)S(1)}, f32[40,80]{1,0:T(8,128)S(1)}, u32[]{:S(2)}, u32[]{:S(2)}) collective-permute-start(f32[40,80]{1,0:T(8,128)S(1)} %get-tuple-element.51), channel_id=1, source_target_pairs={{0,192},{64,0},{128,64},{192,128},{1,193},{65,1},{129,65},{193,129... | collective-permute-start | bytes 38408 | tf_op jit(solution)/shard_map/ppermute | solution.py:495
  107.9 27.4 %collective-permute-start.13 = (f32[24,8,512]{2,1,0:T(8,128)S(1)}, f32[24,8,512]{2,1,0:T(8,128)S(1)}, u32[]{:S(2)}, u32[]{:S(2)}) collective-permute-start(f32[24,8,512]{2,1,0:T(8,128)S(1)} %get-tuple-element.52), channel_id=1, source_target_pairs={{0,1},{1,0},{2,3},{3,2},{4,5},{5,4},{6,7},{7,6},{8,9},{9,8},{10,11... | collective-permute-start | bytes 1179656 | tf_op jit(solution)/shard_map/ppermute | solution.py:455
  108.2 6.3 %collective-permute-start.14 = (f32[40,80]{1,0:T(8,128)S(1)}, f32[40,80]{1,0:T(8,128)S(1)}, u32[]{:S(2)}, u32[]{:S(2)}) collective-permute-start(f32[40,80]{1,0:T(8,128)S(1)} %add_add_fusion.1), channel_id=1, source_target_pairs={{0,4},{1,5},{2,6},{3,7},{4,0},{5,1},{6,2},{7,3},{8,12},{9,13},{10,... | collective-permute-start | bytes 38408 | tf_op jit(solution)/shard_map/ppermute | solution.py:455
  114.6 5.9 %collective-permute-start.15 = (f32[40,80]{1,0:T(8,128)S(1)}, f32[40,80]{1,0:T(8,128)S(1)}, u32[]{:S(2)}, u32[]{:S(2)}) collective-permute-start(f32[40,80]{1,0:T(8,128)S(1)} %add.38), channel_id=1, source_target_pairs={{0,12},{1,13},{2,14},{3,15},{4,8},{5,9},{6,10},{7,11},{8,4},{9,5},... | collective-permute-start | bytes 38408 | tf_op jit(solution)/shard_map/ppermute | solution.py:455
  120.5 3.8 %collective-permute-start.16 = (f32[40,80]{1,0:T(8,128)S(1)}, f32[40,80]{1,0:T(8,128)S(1)}, u32[]{:S(2)}, u32[]{:S(2)}) collective-permute-start(f32[40,80]{1,0:T(8,128)S(1)} %add.39), channel_id=1, source_target_pairs={{0,16},{1,17},{2,18},{3,19},{4,20},{5,21},{6,22},{7,23},{8,24},{9,... | collective-permute-start | bytes 38408 | tf_op jit(solution)/shard_map/ppermute | solution.py:455
  124.2 5.0 %collective-permute-start.17 = (f32[40,80]{1,0:T(8,128)S(1)}, f32[40,80]{1,0:T(8,128)S(1)}, u32[]{:S(2)}, u32[]{:S(2)}) collective-permute-start(f32[40,80]{1,0:T(8,128)S(1)} %add.40), channel_id=1, source_target_pairs={{0,48},{1,49},{2,50},{3,51},{4,52},{5,53},{6,54},{7,55},{8,56},{9,... | collective-permute-start | bytes 38408 | tf_op jit(solution)/shard_map/ppermute | solution.py:455
  129.2 3.8 %collective-permute-start.18 = (f32[40,80]{1,0:T(8,128)S(1)}, f32[40,80]{1,0:T(8,128)S(1)}, u32[]{:S(2)}, u32[]{:S(2)}) collective-permute-start(f32[40,80]{1,0:T(8,128)S(1)} %add.41), channel_id=1, source_target_pairs={{0,1},{1,0},{2,3},{3,2},{4,5},{5,4},{6,7},{7,6},{8,9},{9,8},{10,11... | collective-permute-start | bytes 38408 | tf_op jit(solution)/shard_map/ppermute | solution.py:455
  129.5 3.8 %collective-permute-start.19 = (f32[40,80]{1,0:T(8,128)S(1)}, f32[40,80]{1,0:T(8,128)S(1)}, u32[]{:S(2)}, u32[]{:S(2)}) collective-permute-start(f32[40,80]{1,0:T(8,128)S(1)} %add.41), channel_id=1, source_target_pairs={{0,2},{1,3},{2,0},{3,1},{4,6},{5,7},{6,4},{7,5},{8,10},{9,11},{10,... | collective-permute-start | bytes 38408 | tf_op jit(solution)/shard_map/ppermute | solution.py:455
  129.5 5.2 %collective-permute-start.20 = (f32[40,80]{1,0:T(8,128)S(1)}, f32[40,80]{1,0:T(8,128)S(1)}, u32[]{:S(2)}, u32[]{:S(2)}) collective-permute-start(f32[40,80]{1,0:T(8,128)S(1)} %add.41), channel_id=1, source_target_pairs={{0,3},{1,2},{2,1},{3,0},{4,7},{5,6},{6,5},{7,4},{8,11},{9,10},{10,... | collective-permute-start | bytes 38408 | tf_op jit(solution)/shard_map/ppermute | solution.py:455
  (3 other events, 14.2 us)

commit v3 on v2

--- a/solution.py
+++ b/solution.py
@@ -171,12 +171,9 @@
         p_ref[spot] = begin
 
     for ref, base in zip(strips, strip_bases(side)):
-        def fill_row(row, carry, ref=ref, base=base):
+        for row in range(ROWS):
             for index in range(sets):
                 place(ref[row * sets + index], base + row, (base + row) * sets + index)
-            return carry
-
-        lax.fori_loop(0, ROWS, fill_row, 0)
     for ref, above in zip(far, (side, 1 - side)):
         base = above * (8 - NEAR) + (ALL_ROWS - 8) * (1 - above)
         for row in range(NEAR):
@@ -259,7 +256,7 @@
     side_ref, stiff_ref, dens_ref,
     keep_ref, give_ref, up_ref, dn_ref, far_keep_ref, far_give_ref,
     own_ref, other_ref, frames_ref, fx_ref, fy_ref, fw_ref, mk_ref, mask_ref,
-    p_ref, u_ref, s_ref, m_ref, fs_ref,
+    p_ref, u_ref, s_ref, m_ref,
 ):
     side = side_ref[0]
     strips = [keep_ref, give_ref]
@@ -308,16 +305,11 @@
 
     def keep_row(index, at, spot, mask, fast):
         rows = pl.ds(pl.multiple_of(index * SENS, SENS), SENS)
-        fs_ref[at, rows, 0:WIDE] = p_ref[spot] * mask
-        fs_ref[at, rows, WIDE : 2 * WIDE] = u_ref[spot] * fast
+        frames_ref[at, rows, 0:WIDE] = p_ref[spot] * mask
+        frames_ref[at, rows, WIDE : 2 * WIDE] = u_ref[spot] * fast
 
     march(1, 16, keep_row, mask_ref, p_ref, u_ref, fx_ref, fy_ref, fw_ref, mk_ref)
 
-    def narrow(row, carry):
-        frames_ref[row] = fs_ref[row].astype(jnp.bfloat16)
-        return carry
-
-    lax.fori_loop(0, CENTRE_ROWS, narrow, 0)
     for out_ref, cells in zip((own_ref, other_ref), in_order(side, 1, p_ref)):
         out_ref[...] = cells
 
@@ -347,7 +339,8 @@
     def gram(turn, total):
         for extra in range(4):
             row = 4 * turn + extra
-            total = total + lax.dot_general(fa_ref[row], frames_ref[row], (((1,), (1,)), ((), ())), **FAST)
+            frames = frames_ref[row].astype(jnp.bfloat16)
+            total = total + lax.dot_general(fa_ref[row], frames, (((1,), (1,)), ((), ())), **FAST)
         return total
 
     total = lax.fori_loop(0, CENTRE_ROWS // 4, gram, jnp.zeros((ACT * SNAPS, SENS * SNAPS), jnp.float32))
@@ -409,12 +402,11 @@
     return call(
         sensor_kernel, scalars, operands,
         (
-            part, part, array(CENTRE_ROWS, SENS * SNAPS, 2 * WIDE, dtype=jnp.bfloat16),
+            part, part, array(CENTRE_ROWS, SENS * SNAPS, 2 * WIDE),
             face, face, array(ROOM, 8, LANES), face, array(2, LANES - FLAG_LANE, WIDE),
         ),
         [
             scratch(ROOM, 8, WIDE), scratch(ROOM, 8, WIDE), scratch(ALL_ROWS, WIDE), scratch(ALL_ROWS, WIDE),
-            scratch(CENTRE_ROWS, SENS * SNAPS, 2 * WIDE),
         ],
         28,
     )

time: 137 us -> 136 us (level)
  no operation moved by 1% of the time
where the time goes in v3:
time: 136 us; the launch traced here: 135 us
  waiting for transfers between devices  49 us (36%)
  starting transfers between devices  48.1 us (35%)
  Pallas kernels  35.9 us (26%)
  other arithmetic  1.6 us (1%)
    pallas_call x5, Pallas kernels, call(): pl.pallas_call(kernel, out_shape=out_shape, in_specs=[smem] * len(scalars...  32.7 us
    ppermute x10, waiting for transfers between devices, swap(): return lax.ppermute(cells, 'dom', [(i, i ^ bit) for i in range(count)])  24.2 us
    ppermute x2, waiting for transfers between devices, outward(): lax.ppermute(cells, 'dom', [(i, j) for i, j in pairs if 0 <= j < count])  19.9 us
    ppermute x4, starting transfers between devices, along_dom(): lax.ppermute(cells, 'dom', [(i, i + distance) for i in range(count) if 0...  17.8 us
    ppermute x10, starting transfers between devices, swap(): return lax.ppermute(cells, 'dom', [(i, i ^ bit) for i in range(count)])  10.9 us
    ppermute x3, starting transfers between devices, body(): lax.ppermute(pieces[hop], 'sec', [(i, (i + hop) % sections) for i in rang...  9.97 us
    ppermute x2, starting transfers between devices, outward(): lax.ppermute(cells, 'dom', [(i, j) for i, j in pairs if 0 <= j < count])  6.45 us
    ppermute x1, waiting for transfers between devices, body(): lax.ppermute(left_edge, 'sec', [(i + 1, i) for i in range(sections - 1)])  3.36 us
  transfers between devices with their start and end apart: 21, of which 13 were waited for; matrix products, arithmetic and copies ran while one was open for 0% of the time, Pallas kernels for 11%

profile of v3, /device:TPU:24, one launch (start us, length us, event | category | flops | bytes accessed | tf_op | source)
XLA Modules:
  0.0 135.4 jit_solution(6783405031531600254)
XLA Ops:
  0.7 1.6 %shard_map.78 = (f32[25,8,128]{2,1,0:T(8,128)}, f32[25,8,128]{2,1,0:T(8,128)}) custom-call(f32[16,8,1024]{2,1,0:T(8,128)} %refs_3_.1, f32[8,8,1024]{2,1,0:T(8,128)} %refs_4_.1, s32[8,1024]{1,0:T(8,128)} %refs_5_.1, f32[16,8,1024]{2,1,0:T(8,128)} %refs_3_.1, f32[8,8,1024]{2,1,0:T(8,128)} %refs_4_.1, s32[8,1024]{1,0:T(8,128)} %refs_5_.1), custom_call_target="tpu_custom_call" | custom-call | tf_op jit(solution)/shard_map/pallas_call | solution.py:93
  2.3 1.7 %collective-permute-start = (f32[25,8,128]{2,1,0:T(8,128)}, f32[25,8,128]{2,1,0:T(8,128)S(1)}, u32[]{:S(2)}, u32[]{:S(2)}) collective-permute-start(f32[25,8,128]{2,1,0:T(8,128)} %get-tuple-element.30), channel_id=1, source_target_pairs={{0,64},{64,128},{128,192},{1,65},{65,129},{129,193},{2,66},{66,130... | collective-permute-start | bytes 307208 | tf_op jit(solution)/shard_map/ppermute | solution.py:456
  5.4 1.5 %shard_map.77 = (f32[25,8,640]{2,1,0:T(8,128)S(1)}, f32[25,8,640]{2,1,0:T(8,128)S(1)}) custom-call(f32[16,8,1024]{2,1,0:T(8,128)S(1)} %copy-done, f32[8,8,1024]{2,1,0:T(8,128)S(1)} %copy-done.1, s32[8,1024]{1,0:T(8,128)S(1)} %copy-done.2, s32[8,10]{1,0:T(8,128)S(1)} %bitcast.5), custom_call_target="tpu_custom_call" | custom-call | tf_op jit(solution)/shard_map/pallas_call | solution.py:463
  6.9 3.4 %collective-permute-done.1.right_ref = f32[25,8,128]{2,1,0:T(8,128)S(1)} collective-permute-done((f32[25,8,128]{2,1,0:T(8,128)}, f32[25,8,128]{2,1,0:T(8,128)S(1)}, u32[]{:S(2)}, u32[]{:S(2)}) %collective-permute-start.1) | collective-permute-done | bytes 102432 | tf_op jit(solution)/shard_map/ppermute | solution.py:457
  12.3 6.5 %collective-permute-done.2.second_ref.give_ref = f32[16,8,640]{2,1,0:T(8,128)S(1)} collective-permute-done((f32[16,8,640]{2,1,0:T(8,128)S(1)}, f32[16,8,640]{2,1,0:T(8,128)S(1)}, u32[]{:S(2)}, u32[]{:S(2)}) %collective-permute-start.2) | collective-permute-done | bytes 327712 | tf_op jit(solution)/shard_map/ppermute | solution.py:447
  18.9 3.8 %collective-permute-start.3 = (f32[32,8,640]{2,1,0:T(8,128)S(1)}, f32[32,8,640]{2,1,0:T(8,128)S(1)}, u32[]{:S(2)}, u32[]{:S(2)}) collective-permute-start(f32[32,8,640]{2,1,0:T(8,128)S(1)} %shard_map.80), channel_id=1, source_target_pairs={{0,2},{1,3},{2,4},{3,5},{4,6},{5,7},{6,8},{7,9},{8,10},{9,11},{10,... | collective-permute-start | bytes 1966088 | tf_op jit(solution)/shard_map/ppermute | solution.py:432
  22.7 6.0 %collective-permute-start.4 = (f32[32,8,640]{2,1,0:T(8,128)S(1)}, f32[32,8,640]{2,1,0:T(8,128)S(1)}, u32[]{:S(2)}, u32[]{:S(2)}) collective-permute-start(f32[32,8,640]{2,1,0:T(8,128)S(1)} %shard_map.80), channel_id=1, source_target_pairs={{2,0},{3,1},{4,2},{5,3},{6,4},{7,5},{8,6},{9,7},{10,8},{11,9},{12,... | collective-permute-start | bytes 1966088 | tf_op jit(solution)/shard_map/ppermute | solution.py:432
  29.4 4.3 %collective-permute-start.5 = (f32[10,8,640]{2,1,0:T(8,128)S(1)}, f32[10,8,640]{2,1,0:T(8,128)S(1)}, u32[]{:S(2)}, u32[]{:S(2)}) collective-permute-start(f32[10,8,640]{2,1,0:T(8,128)S(1)} %get-tuple-element.34), channel_id=1, source_target_pairs={{1,5},{3,7},{4,0},{5,9},{6,2},{7,11},{8,4},{9,13},{10,6},{11,15},{... | collective-permute-start | bytes 614408 | tf_op jit(solution)/shard_map/ppermute | solution.py:438
  35.1 2.3 %collective-permute-start.8 = (f32[18,8,640]{2,1,0:T(8,128)}, f32[18,8,640]{2,1,0:T(8,128)}, u32[]{:S(2)}, u32[]{:S(2)}) collective-permute-start(f32[18,8,640]{2,1,0:T(8,128)} %shard_map.81), channel_id=1, source_target_pairs={{0,2},{1,3},{2,4},{3,5},{4,6},{5,7},{6,8},{7,9},{8,10},{9,11},{10,... | collective-permute-start | bytes 1105928 | tf_op jit(solution)/shard_map/ppermute | solution.py:432
  37.5 5.6 %collective-permute-start.9 = (f32[18,8,640]{2,1,0:T(8,128)}, f32[18,8,640]{2,1,0:T(8,128)}, u32[]{:S(2)}, u32[]{:S(2)}) collective-permute-start(f32[18,8,640]{2,1,0:T(8,128)} %shard_map.81), channel_id=1, source_target_pairs={{2,0},{3,1},{4,2},{5,3},{6,4},{7,5},{8,6},{9,7},{10,8},{11,9},{12,... | collective-permute-start | bytes 1105928 | tf_op jit(solution)/shard_map/ppermute | solution.py:432
  43.1 3.9 %collective-permute-done.5.far_keep_ref = f32[10,8,640]{2,1,0:T(8,128)S(1)} collective-permute-done((f32[10,8,640]{2,1,0:T(8,128)S(1)}, f32[10,8,640]{2,1,0:T(8,128)S(1)}, u32[]{:S(2)}, u32[]{:S(2)}) %collective-permute-start.5) | collective-permute-done | bytes 204832 | tf_op jit(solution)/shard_map/ppermute | solution.py:438
  47.0 2.1 %collective-permute-start.6 = (f32[10,8,640]{2,1,0:T(8,128)}, f32[10,8,640]{2,1,0:T(8,128)S(1)}, u32[]{:S(2)}, u32[]{:S(2)}) collective-permute-start(f32[10,8,640]{2,1,0:T(8,128)} %get-tuple-element.35), channel_id=1, source_target_pairs={{1,4},{3,6},{4,1},{5,8},{6,3},{7,10},{8,5},{9,12},{10,7},{11,14},{... | collective-permute-start | bytes 614408 | tf_op jit(solution)/shard_map/ppermute | solution.py:438
  49.1 16.0 %collective-permute-done.6.far_give_ref = f32[10,8,640]{2,1,0:T(8,128)S(1)} collective-permute-done((f32[10,8,640]{2,1,0:T(8,128)}, f32[10,8,640]{2,1,0:T(8,128)S(1)}, u32[]{:S(2)}, u32[]{:S(2)}) %collective-permute-start.6) | collective-permute-done | bytes 204832 | tf_op jit(solution)/shard_map/ppermute | solution.py:438
  65.2 12.0 %shard_map.82 = (f32[8,8,512]{2,1,0:T(8,128)S(1)}, f32[8,8,512]{2,1,0:T(8,128)S(1)}, f32[16,80,1280]{2,1,0:T(8,128)S(1)}, f32[80,8,640]{2,1,0:T(8,128)S(1)}, f32...) custom-call(s32[1]{0:T(128)} %bitcast.side_ref, ...), custom_call_target="tpu_custom_call" | custom-call | tf_op jit(solution)/shard_map/pallas_call | solution.py:378
  77.2 18.4 %shard_map.83 = (f32[24,8,512]{2,1,0:T(8,128)S(1)}, f32[24,8,512]{2,1,0:T(8,128)S(1)}, f32[40,80]{1,0:T(8,128)S(1)}, f32[40,80]{1,0:T(8,128)S(1)}, f32[40,80]{1,0:T(8,128)S(1)}, /*index=5*/f32[40,80]{1,0:T(8,128)S(1)}) custom-call(s32[1]{0:T(128)} %bitcast.side_ref, s32[1]{0:T(128)} %bitcast.1.place_ref, ...), custom_call_target="tpu_custom_call" | custom-call | tf_op jit(solution)/shard_map/pallas_call | solution.py:378
  95.6 4.5 %collective-permute-start.10 = (f32[40,80]{1,0:T(8,128)S(1)}, f32[40,80]{1,0:T(8,128)S(1)}, u32[]{:S(2)}, u32[]{:S(2)}) collective-permute-start(f32[40,80]{1,0:T(8,128)S(1)} %get-tuple-element.49), channel_id=1, source_target_pairs={{0,64},{64,128},{128,192},{192,0},{1,65},{65,129},{129,193},{193,1... | collective-permute-start | bytes 38408 | tf_op jit(solution)/shard_map/ppermute | solution.py:487
  100.1 2.6 %collective-permute-start.11 = (f32[40,80]{1,0:T(8,128)S(1)}, f32[40,80]{1,0:T(8,128)S(1)}, u32[]{:S(2)}, u32[]{:S(2)}) collective-permute-start(f32[40,80]{1,0:T(8,128)S(1)} %get-tuple-element.50), channel_id=1, source_target_pairs={{0,128},{64,192},{128,0},{192,64},{1,129},{65,193},{129,1},{193,65... | collective-permute-start | bytes 38408 | tf_op jit(solution)/shard_map/ppermute | solution.py:487
  102.7 2.9 %collective-permute-start.12 = (f32[40,80]{1,0:T(8,128)S(1)}, f32[40,80]{1,0:T(8,128)S(1)}, u32[]{:S(2)}, u32[]{:S(2)}) collective-permute-start(f32[40,80]{1,0:T(8,128)S(1)} %get-tuple-element.51), channel_id=1, source_target_pairs={{0,192},{64,0},{128,64},{192,128},{1,193},{65,1},{129,65},{193,129... | collective-permute-start | bytes 38408 | tf_op jit(solution)/shard_map/ppermute | solution.py:487
  107.4 4.6 %collective-permute-start.14 = (f32[40,80]{1,0:T(8,128)S(1)}, f32[40,80]{1,0:T(8,128)S(1)}, u32[]{:S(2)}, u32[]{:S(2)}) collective-permute-start(f32[40,80]{1,0:T(8,128)S(1)} %add_add_fusion.1), channel_id=1, source_target_pairs={{0,4},{1,5},{2,6},{3,7},{4,0},{5,1},{6,2},{7,3},{8,12},{9,13},{10,... | collective-permute-start | bytes 38408 | tf_op jit(solution)/shard_map/ppermute | solution.py:447
  111.9 1.8 %collective-permute-done.14 = f32[40,80]{1,0:T(8,128)S(1)} collective-permute-done((f32[40,80]{1,0:T(8,128)S(1)}, f32[40,80]{1,0:T(8,128)S(1)}, u32[]{:S(2)}, u32[]{:S(2)}) %collective-permute-start.14) | collective-permute-done | bytes 12832 | tf_op jit(solution)/shard_map/ppermute | solution.py:447
  114.0 5.6 %collective-permute-done.15 = f32[40,80]{1,0:T(8,128)S(1)} collective-permute-done((f32[40,80]{1,0:T(8,128)S(1)}, f32[40,80]{1,0:T(8,128)S(1)}, u32[]{:S(2)}, u32[]{:S(2)}) %collective-permute-start.15) | collective-permute-done | bytes 12832 | tf_op jit(solution)/shard_map/ppermute | solution.py:447
  120.3 3.0 %collective-permute-done.16 = f32[40,80]{1,0:T(8,128)S(1)} collective-permute-done((f32[40,80]{1,0:T(8,128)S(1)}, f32[40,80]{1,0:T(8,128)S(1)}, u32[]{:S(2)}, u32[]{:S(2)}) %collective-permute-start.16) | collective-permute-done | bytes 12832 | tf_op jit(solution)/shard_map/ppermute | solution.py:447
  123.6 4.7 %collective-permute-done.17 = f32[40,80]{1,0:T(8,128)S(1)} collective-permute-done((f32[40,80]{1,0:T(8,128)S(1)}, f32[40,80]{1,0:T(8,128)S(1)}, u32[]{:S(2)}, u32[]{:S(2)}) %collective-permute-start.17) | collective-permute-done | bytes 12832 | tf_op jit(solution)/shard_map/ppermute | solution.py:447
  128.7 3.2 %collective-permute-start.20 = (f32[40,80]{1,0:T(8,128)S(1)}, f32[40,80]{1,0:T(8,128)S(1)}, u32[]{:S(2)}, u32[]{:S(2)}) collective-permute-start(f32[40,80]{1,0:T(8,128)S(1)} %add.41), channel_id=1, source_target_pairs={{0,3},{1,2},{2,1},{3,0},{4,7},{5,6},{6,5},{7,4},{8,11},{9,10},{10,... | collective-permute-start | bytes 38408 | tf_op jit(solution)/shard_map/ppermute | solution.py:447
  (44 shorter events, 12.4 us)
Async XLA Ops:
  0.6 4.7 %copy-start = (f32[16,8,1024]{2,1,0:T(8,128)S(1)}, f32[16,8,1024]{2,1,0:T(8,128)}, u32[]{:S(2)}) copy-start(f32[16,8,1024]{2,1,0:T(8,128)} %refs_3_.1) | copy-start | bytes 1572868
  2.3 4.6 %collective-permute-start = (f32[25,8,128]{2,1,0:T(8,128)}, f32[25,8,128]{2,1,0:T(8,128)S(1)}, u32[]{:S(2)}, u32[]{:S(2)}) collective-permute-start(f32[25,8,128]{2,1,0:T(8,128)} %get-tuple-element.30), channel_id=1, source_target_pairs={{0,64},{64,128},{128,192},{1,65},{65,129},{129,193},{2,66},{66,130... | collective-permute-start | bytes 307208 | tf_op jit(solution)/shard_map/ppermute | solution.py:456
  4.1 6.2 %collective-permute-start.1 = (f32[25,8,128]{2,1,0:T(8,128)}, f32[25,8,128]{2,1,0:T(8,128)S(1)}, u32[]{:S(2)}, u32[]{:S(2)}) collective-permute-start(f32[25,8,128]{2,1,0:T(8,128)} %get-tuple-element.31), channel_id=1, source_target_pairs={{64,0},{128,64},{192,128},{65,1},{129,65},{193,129},{66,2},{130,66... | collective-permute-start | bytes 307208 | tf_op jit(solution)/shard_map/ppermute | solution.py:457
  10.3 54.9 %copy-start.4 = (f32[16]{0:T(128)S(1)}, f32[16]{0:T(128)}, u32[]{:S(2)}) copy-start(f32[16]{0:T(128)} %stiff_ref.1) | copy-start | bytes 196
  10.3 54.9 %copy-start.5 = (f32[16]{0:T(128)S(1)}, f32[16]{0:T(128)}, u32[]{:S(2)}) copy-start(f32[16]{0:T(128)} %dens_ref.1) | copy-start | bytes 196
  11.8 7.1 %collective-permute-start.2 = (f32[16,8,640]{2,1,0:T(8,128)S(1)}, f32[16,8,640]{2,1,0:T(8,128)S(1)}, u32[]{:S(2)}, u32[]{:S(2)}) collective-permute-start(f32[16,8,640]{2,1,0:T(8,128)S(1)} %get-tuple-element.33), channel_id=1, source_target_pairs={{0,1},{1,0},{2,3},{3,2},{4,5},{5,4},{6,7},{7,6},{8,9},{9,8},{10,11... | collective-permute-start | bytes 983048 | tf_op jit(solution)/shard_map/ppermute | solution.py:447
  18.9 58.3 %collective-permute-start.3 = (f32[32,8,640]{2,1,0:T(8,128)S(1)}, f32[32,8,640]{2,1,0:T(8,128)S(1)}, u32[]{:S(2)}, u32[]{:S(2)}) collective-permute-start(f32[32,8,640]{2,1,0:T(8,128)S(1)} %shard_map.80), channel_id=1, source_target_pairs={{0,2},{1,3},{2,4},{3,5},{4,6},{5,7},{6,8},{7,9},{8,10},{9,11},{10,... | collective-permute-start | bytes 1966088 | tf_op jit(solution)/shard_map/ppermute | solution.py:432
  22.7 54.4 %collective-permute-start.4 = (f32[32,8,640]{2,1,0:T(8,128)S(1)}, f32[32,8,640]{2,1,0:T(8,128)S(1)}, u32[]{:S(2)}, u32[]{:S(2)}) collective-permute-start(f32[32,8,640]{2,1,0:T(8,128)S(1)} %shard_map.80), channel_id=1, source_target_pairs={{2,0},{3,1},{4,2},{5,3},{6,4},{7,5},{8,6},{9,7},{10,8},{11,9},{12,... | collective-permute-start | bytes 1966088 | tf_op jit(solution)/shard_map/ppermute | solution.py:432
  28.8 5.6 %collective-permute-start.7 = (f32[9,8,640]{2,1,0:T(8,128)S(1)}, f32[9,8,640]{2,1,0:T(8,128)S(1)}, u32[]{:S(2)}, u32[]{:S(2)}) collective-permute-start(f32[9,8,640]{2,1,0:T(8,128)S(1)} %get-tuple-element.37), channel_id=1, source_target_pairs={{0,1},{1,0},{2,3},{3,2},{4,5},{5,4},{6,7},{7,6},{8,9},{9,8},{10,11... | collective-permute-start | bytes 552968 | tf_op jit(solution)/shard_map/ppermute | solution.py:447
  29.4 17.6 %collective-permute-start.5 = (f32[10,8,640]{2,1,0:T(8,128)S(1)}, f32[10,8,640]{2,1,0:T(8,128)S(1)}, u32[]{:S(2)}, u32[]{:S(2)}) collective-permute-start(f32[10,8,640]{2,1,0:T(8,128)S(1)} %get-tuple-element.34), channel_id=1, source_target_pairs={{1,5},{3,7},{4,0},{5,9},{6,2},{7,11},{8,4},{9,13},{10,6},{11,15},{... | collective-permute-start | bytes 614408 | tf_op jit(solution)/shard_map/ppermute | solution.py:438
  35.1 30.0 %collective-permute-start.8 = (f32[18,8,640]{2,1,0:T(8,128)}, f32[18,8,640]{2,1,0:T(8,128)}, u32[]{:S(2)}, u32[]{:S(2)}) collective-permute-start(f32[18,8,640]{2,1,0:T(8,128)} %shard_map.81), channel_id=1, source_target_pairs={{0,2},{1,3},{2,4},{3,5},{4,6},{5,7},{6,8},{7,9},{8,10},{9,11},{10,... | collective-permute-start | bytes 1105928 | tf_op jit(solution)/shard_map/ppermute | solution.py:432
  37.5 27.6 %collective-permute-start.9 = (f32[18,8,640]{2,1,0:T(8,128)}, f32[18,8,640]{2,1,0:T(8,128)}, u32[]{:S(2)}, u32[]{:S(2)}) collective-permute-start(f32[18,8,640]{2,1,0:T(8,128)} %shard_map.81), channel_id=1, source_target_pairs={{2,0},{3,1},{4,2},{5,3},{6,4},{7,5},{8,6},{9,7},{10,8},{11,9},{12,... | collective-permute-start | bytes 1105928 | tf_op jit(solution)/shard_map/ppermute | solution.py:432
  47.0 18.1 %collective-permute-start.6 = (f32[10,8,640]{2,1,0:T(8,128)}, f32[10,8,640]{2,1,0:T(8,128)S(1)}, u32[]{:S(2)}, u32[]{:S(2)}) collective-permute-start(f32[10,8,640]{2,1,0:T(8,128)} %get-tuple-element.35), channel_id=1, source_target_pairs={{1,4},{3,6},{4,1},{5,8},{6,3},{7,10},{8,5},{9,12},{10,7},{11,14},{... | collective-permute-start | bytes 614408 | tf_op jit(solution)/shard_map/ppermute | solution.py:438
  95.6 10.0 %collective-permute-start.10 = (f32[40,80]{1,0:T(8,128)S(1)}, f32[40,80]{1,0:T(8,128)S(1)}, u32[]{:S(2)}, u32[]{:S(2)}) collective-permute-start(f32[40,80]{1,0:T(8,128)S(1)} %get-tuple-element.49), channel_id=1, source_target_pairs={{0,64},{64,128},{128,192},{192,0},{1,65},{65,129},{129,193},{193,1... | collective-permute-start | bytes 38408 | tf_op jit(solution)/shard_map/ppermute | solution.py:487
  100.1 5.5 %collective-permute-start.11 = (f32[40,80]{1,0:T(8,128)S(1)}, f32[40,80]{1,0:T(8,128)S(1)}, u32[]{:S(2)}, u32[]{:S(2)}) collective-permute-start(f32[40,80]{1,0:T(8,128)S(1)} %get-tuple-element.50), channel_id=1, source_target_pairs={{0,128},{64,192},{128,0},{192,64},{1,129},{65,193},{129,1},{193,65... | collective-permute-start | bytes 38408 | tf_op jit(solution)/shard_map/ppermute | solution.py:487
  102.7 4.4 %collective-permute-start.12 = (f32[40,80]{1,0:T(8,128)S(1)}, f32[40,80]{1,0:T(8,128)S(1)}, u32[]{:S(2)}, u32[]{:S(2)}) collective-permute-start(f32[40,80]{1,0:T(8,128)S(1)} %get-tuple-element.51), channel_id=1, source_target_pairs={{0,192},{64,0},{128,64},{192,128},{1,193},{65,1},{129,65},{193,129... | collective-permute-start | bytes 38408 | tf_op jit(solution)/shard_map/ppermute | solution.py:487
  107.1 27.4 %collective-permute-start.13 = (f32[24,8,512]{2,1,0:T(8,128)S(1)}, f32[24,8,512]{2,1,0:T(8,128)S(1)}, u32[]{:S(2)}, u32[]{:S(2)}) collective-permute-start(f32[24,8,512]{2,1,0:T(8,128)S(1)} %get-tuple-element.52), channel_id=1, source_target_pairs={{0,1},{1,0},{2,3},{3,2},{4,5},{5,4},{6,7},{7,6},{8,9},{9,8},{10,11... | collective-permute-start | bytes 1179656 | tf_op jit(solution)/shard_map/ppermute | solution.py:447
  107.4 6.3 %collective-permute-start.14 = (f32[40,80]{1,0:T(8,128)S(1)}, f32[40,80]{1,0:T(8,128)S(1)}, u32[]{:S(2)}, u32[]{:S(2)}) collective-permute-start(f32[40,80]{1,0:T(8,128)S(1)} %add_add_fusion.1), channel_id=1, source_target_pairs={{0,4},{1,5},{2,6},{3,7},{4,0},{5,1},{6,2},{7,3},{8,12},{9,13},{10,... | collective-permute-start | bytes 38408 | tf_op jit(solution)/shard_map/ppermute | solution.py:447
  113.7 5.9 %collective-permute-start.15 = (f32[40,80]{1,0:T(8,128)S(1)}, f32[40,80]{1,0:T(8,128)S(1)}, u32[]{:S(2)}, u32[]{:S(2)}) collective-permute-start(f32[40,80]{1,0:T(8,128)S(1)} %add.38), channel_id=1, source_target_pairs={{0,12},{1,13},{2,14},{3,15},{4,8},{5,9},{6,10},{7,11},{8,4},{9,5},... | collective-permute-start | bytes 38408 | tf_op jit(solution)/shard_map/ppermute | solution.py:447
  119.6 3.8 %collective-permute-start.16 = (f32[40,80]{1,0:T(8,128)S(1)}, f32[40,80]{1,0:T(8,128)S(1)}, u32[]{:S(2)}, u32[]{:S(2)}) collective-permute-start(f32[40,80]{1,0:T(8,128)S(1)} %add.39), channel_id=1, source_target_pairs={{0,16},{1,17},{2,18},{3,19},{4,20},{5,21},{6,22},{7,23},{8,24},{9,... | collective-permute-start | bytes 38408 | tf_op jit(solution)/shard_map/ppermute | solution.py:447
  123.4 5.0 %collective-permute-start.17 = (f32[40,80]{1,0:T(8,128)S(1)}, f32[40,80]{1,0:T(8,128)S(1)}, u32[]{:S(2)}, u32[]{:S(2)}) collective-permute-start(f32[40,80]{1,0:T(8,128)S(1)} %add.40), channel_id=1, source_target_pairs={{0,48},{1,49},{2,50},{3,51},{4,52},{5,53},{6,54},{7,55},{8,56},{9,... | collective-permute-start | bytes 38408 | tf_op jit(solution)/shard_map/ppermute | solution.py:447
  128.4 3.8 %collective-permute-start.18 = (f32[40,80]{1,0:T(8,128)S(1)}, f32[40,80]{1,0:T(8,128)S(1)}, u32[]{:S(2)}, u32[]{:S(2)}) collective-permute-start(f32[40,80]{1,0:T(8,128)S(1)} %add.41), channel_id=1, source_target_pairs={{0,1},{1,0},{2,3},{3,2},{4,5},{5,4},{6,7},{7,6},{8,9},{9,8},{10,11... | collective-permute-start | bytes 38408 | tf_op jit(solution)/shard_map/ppermute | solution.py:447
  128.7 3.8 %collective-permute-start.19 = (f32[40,80]{1,0:T(8,128)S(1)}, f32[40,80]{1,0:T(8,128)S(1)}, u32[]{:S(2)}, u32[]{:S(2)}) collective-permute-start(f32[40,80]{1,0:T(8,128)S(1)} %add.41), channel_id=1, source_target_pairs={{0,2},{1,3},{2,0},{3,1},{4,6},{5,7},{6,4},{7,5},{8,10},{9,11},{10,... | collective-permute-start | bytes 38408 | tf_op jit(solution)/shard_map/ppermute | solution.py:447
  128.7 5.2 %collective-permute-start.20 = (f32[40,80]{1,0:T(8,128)S(1)}, f32[40,80]{1,0:T(8,128)S(1)}, u32[]{:S(2)}, u32[]{:S(2)}) collective-permute-start(f32[40,80]{1,0:T(8,128)S(1)} %add.41), channel_id=1, source_target_pairs={{0,3},{1,2},{2,1},{3,0},{4,7},{5,6},{6,5},{7,4},{8,11},{9,10},{10,... | collective-permute-start | bytes 38408 | tf_op jit(solution)/shard_map/ppermute | solution.py:447
  (3 other events, 14.2 us)

commit v4 on v3

--- a/solution.py
+++ b/solution.py
@@ -337,13 +337,13 @@
     march(ACT_SETS, 6, keep_row, mask_ref, p_ref, u_ref, fx_ref, fy_ref, fw_ref, mk_ref)
 
     def gram(turn, total):
-        for extra in range(4):
-            row = 4 * turn + extra
+        for extra in range(8):
+            row = 8 * turn + extra
             frames = frames_ref[row].astype(jnp.bfloat16)
             total = total + lax.dot_general(fa_ref[row], frames, (((1,), (1,)), ((), ())), **FAST)
         return total
 
-    total = lax.fori_loop(0, CENTRE_ROWS // 4, gram, jnp.zeros((ACT * SNAPS, SENS * SNAPS), jnp.float32))
+    total = lax.fori_loop(0, CENTRE_ROWS // 8, gram, jnp.zeros((ACT * SNAPS, SENS * SNAPS), jnp.float32))
     shape = (ACT * SNAPS, ACT * SNAPS)
     old = lax.broadcasted_iota(jnp.int32, shape, 1)
     new = lax.broadcasted_iota(jnp.int32, shape, 0)

time: 136 us -> 135 us (level)
  no operation moved by 1% of the time
where the time goes in v4:
time: 135 us
  waiting for transfers between devices  49 us (36%)
  starting transfers between devices  48.2 us (36%)
  Pallas kernels  35.6 us (26%)
  other arithmetic  1.6 us (1%)
    pallas_call x5, Pallas kernels, call(): pl.pallas_call(kernel, out_shape=out_shape, in_specs=[smem] * len(scalars...  32.4 us
    ppermute x10, waiting for transfers between devices, swap(): return lax.ppermute(cells, 'dom', [(i, i ^ bit) for i in range(count)])  24.2 us
    ppermute x2, waiting for transfers between devices, outward(): lax.ppermute(cells, 'dom', [(i, j) for i, j in pairs if 0 <= j < count])  19.9 us
    ppermute x4, starting transfers between devices, along_dom(): lax.ppermute(cells, 'dom', [(i, i + distance) for i in range(count) if 0...  17.8 us
    ppermute x10, starting transfers between devices, swap(): return lax.ppermute(cells, 'dom', [(i, i ^ bit) for i in range(count)])  10.9 us
    ppermute x3, starting transfers between devices, body(): lax.ppermute(pieces[hop], 'sec', [(i, (i + hop) % sections) for i in rang...  9.97 us
    ppermute x2, starting transfers between devices, outward(): lax.ppermute(cells, 'dom', [(i, j) for i, j in pairs if 0 <= j < count])  6.47 us
    ppermute x1, waiting for transfers between devices, body(): lax.ppermute(left_edge, 'sec', [(i + 1, i) for i in range(sections - 1)])  3.35 us
  transfers between devices with their start and end apart: 21, of which 13 were waited for; matrix products, arithmetic and copies ran while one was open for 0% of the time, Pallas kernels for 11%

profile of v4, /device:TPU:24, one launch (start us, length us, event | category | flops | bytes accessed | tf_op | source)
XLA Modules:
  0.0 135.1 jit_solution(11178458709001723155)
XLA Ops:
  0.7 1.6 %shard_map.78 = (f32[25,8,128]{2,1,0:T(8,128)}, f32[25,8,128]{2,1,0:T(8,128)}) custom-call(f32[16,8,1024]{2,1,0:T(8,128)} %refs_3_.1, f32[8,8,1024]{2,1,0:T(8,128)} %refs_4_.1, s32[8,1024]{1,0:T(8,128)} %refs_5_.1, f32[16,8,1024]{2,1,0:T(8,128)} %refs_3_.1, f32[8,8,1024]{2,1,0:T(8,128)} %refs_4_.1, s32[8,1024]{1,0:T(8,128)} %refs_5_.1), custom_call_target="tpu_custom_call" | custom-call | tf_op jit(solution)/shard_map/pallas_call | solution.py:93
  2.3 1.7 %collective-permute-start = (f32[25,8,128]{2,1,0:T(8,128)}, f32[25,8,128]{2,1,0:T(8,128)S(1)}, u32[]{:S(2)}, u32[]{:S(2)}) collective-permute-start(f32[25,8,128]{2,1,0:T(8,128)} %get-tuple-element.30), channel_id=1, source_target_pairs={{0,64},{64,128},{128,192},{1,65},{65,129},{129,193},{2,66},{66,130... | collective-permute-start | bytes 307208 | tf_op jit(solution)/shard_map/ppermute | solution.py:456
  5.4 1.5 %shard_map.77 = (f32[25,8,640]{2,1,0:T(8,128)S(1)}, f32[25,8,640]{2,1,0:T(8,128)S(1)}) custom-call(f32[16,8,1024]{2,1,0:T(8,128)S(1)} %copy-done, f32[8,8,1024]{2,1,0:T(8,128)S(1)} %copy-done.1, s32[8,1024]{1,0:T(8,128)S(1)} %copy-done.2, s32[8,10]{1,0:T(8,128)S(1)} %bitcast.5), custom_call_target="tpu_custom_call" | custom-call | tf_op jit(solution)/shard_map/pallas_call | solution.py:463
  6.9 3.4 %collective-permute-done.1.right_ref = f32[25,8,128]{2,1,0:T(8,128)S(1)} collective-permute-done((f32[25,8,128]{2,1,0:T(8,128)}, f32[25,8,128]{2,1,0:T(8,128)S(1)}, u32[]{:S(2)}, u32[]{:S(2)}) %collective-permute-start.1) | collective-permute-done | bytes 102432 | tf_op jit(solution)/shard_map/ppermute | solution.py:457
  12.4 6.5 %collective-permute-done.2.second_ref.give_ref = f32[16,8,640]{2,1,0:T(8,128)S(1)} collective-permute-done((f32[16,8,640]{2,1,0:T(8,128)S(1)}, f32[16,8,640]{2,1,0:T(8,128)S(1)}, u32[]{:S(2)}, u32[]{:S(2)}) %collective-permute-start.2) | collective-permute-done | bytes 327712 | tf_op jit(solution)/shard_map/ppermute | solution.py:447
  18.9 3.8 %collective-permute-start.3 = (f32[32,8,640]{2,1,0:T(8,128)S(1)}, f32[32,8,640]{2,1,0:T(8,128)S(1)}, u32[]{:S(2)}, u32[]{:S(2)}) collective-permute-start(f32[32,8,640]{2,1,0:T(8,128)S(1)} %shard_map.80), channel_id=1, source_target_pairs={{0,2},{1,3},{2,4},{3,5},{4,6},{5,7},{6,8},{7,9},{8,10},{9,11},{10,... | collective-permute-start | bytes 1966088 | tf_op jit(solution)/shard_map/ppermute | solution.py:432
  22.7 6.0 %collective-permute-start.4 = (f32[32,8,640]{2,1,0:T(8,128)S(1)}, f32[32,8,640]{2,1,0:T(8,128)S(1)}, u32[]{:S(2)}, u32[]{:S(2)}) collective-permute-start(f32[32,8,640]{2,1,0:T(8,128)S(1)} %shard_map.80), channel_id=1, source_target_pairs={{2,0},{3,1},{4,2},{5,3},{6,4},{7,5},{8,6},{9,7},{10,8},{11,9},{12,... | collective-permute-start | bytes 1966088 | tf_op jit(solution)/shard_map/ppermute | solution.py:432
  29.4 4.4 %collective-permute-start.5 = (f32[10,8,640]{2,1,0:T(8,128)S(1)}, f32[10,8,640]{2,1,0:T(8,128)S(1)}, u32[]{:S(2)}, u32[]{:S(2)}) collective-permute-start(f32[10,8,640]{2,1,0:T(8,128)S(1)} %get-tuple-element.34), channel_id=1, source_target_pairs={{1,5},{3,7},{4,0},{5,9},{6,2},{7,11},{8,4},{9,13},{10,6},{11,15},{... | collective-permute-start | bytes 614408 | tf_op jit(solution)/shard_map/ppermute | solution.py:438
  35.1 2.3 %collective-permute-start.8 = (f32[18,8,640]{2,1,0:T(8,128)}, f32[18,8,640]{2,1,0:T(8,128)}, u32[]{:S(2)}, u32[]{:S(2)}) collective-permute-start(f32[18,8,640]{2,1,0:T(8,128)} %shard_map.81), channel_id=1, source_target_pairs={{0,2},{1,3},{2,4},{3,5},{4,6},{5,7},{6,8},{7,9},{8,10},{9,11},{10,... | collective-permute-start | bytes 1105928 | tf_op jit(solution)/shard_map/ppermute | solution.py:432
  37.5 5.6 %collective-permute-start.9 = (f32[18,8,640]{2,1,0:T(8,128)}, f32[18,8,640]{2,1,0:T(8,128)}, u32[]{:S(2)}, u32[]{:S(2)}) collective-permute-start(f32[18,8,640]{2,1,0:T(8,128)} %shard_map.81), channel_id=1, source_target_pairs={{2,0},{3,1},{4,2},{5,3},{6,4},{7,5},{8,6},{9,7},{10,8},{11,9},{12,... | collective-permute-start | bytes 1105928 | tf_op jit(solution)/shard_map/ppermute | solution.py:432
  43.1 3.9 %collective-permute-done.5.far_keep_ref = f32[10,8,640]{2,1,0:T(8,128)S(1)} collective-permute-done((f32[10,8,640]{2,1,0:T(8,128)S(1)}, f32[10,8,640]{2,1,0:T(8,128)S(1)}, u32[]{:S(2)}, u32[]{:S(2)}) %collective-permute-start.5) | collective-permute-done | bytes 204832 | tf_op jit(solution)/shard_map/ppermute | solution.py:438
  47.0 2.1 %collective-permute-start.6 = (f32[10,8,640]{2,1,0:T(8,128)}, f32[10,8,640]{2,1,0:T(8,128)S(1)}, u32[]{:S(2)}, u32[]{:S(2)}) collective-permute-start(f32[10,8,640]{2,1,0:T(8,128)} %get-tuple-element.35), channel_id=1, source_target_pairs={{1,4},{3,6},{4,1},{5,8},{6,3},{7,10},{8,5},{9,12},{10,7},{11,14},{... | collective-permute-start | bytes 614408 | tf_op jit(solution)/shard_map/ppermute | solution.py:438
  49.1 16.0 %collective-permute-done.6.far_give_ref = f32[10,8,640]{2,1,0:T(8,128)S(1)} collective-permute-done((f32[10,8,640]{2,1,0:T(8,128)}, f32[10,8,640]{2,1,0:T(8,128)S(1)}, u32[]{:S(2)}, u32[]{:S(2)}) %collective-permute-start.6) | collective-permute-done | bytes 204832 | tf_op jit(solution)/shard_map/ppermute | solution.py:438
  65.1 12.0 %shard_map.82 = (f32[8,8,512]{2,1,0:T(8,128)S(1)}, f32[8,8,512]{2,1,0:T(8,128)S(1)}, f32[16,80,1280]{2,1,0:T(8,128)S(1)}, f32[80,8,640]{2,1,0:T(8,128)S(1)}, f32...) custom-call(s32[1]{0:T(128)} %bitcast.side_ref, ...), custom_call_target="tpu_custom_call" | custom-call | tf_op jit(solution)/shard_map/pallas_call | solution.py:378
  77.2 18.1 %shard_map.83 = (f32[24,8,512]{2,1,0:T(8,128)S(1)}, f32[24,8,512]{2,1,0:T(8,128)S(1)}, f32[40,80]{1,0:T(8,128)S(1)}, f32[40,80]{1,0:T(8,128)S(1)}, f32[40,80]{1,0:T(8,128)S(1)}, /*index=5*/f32[40,80]{1,0:T(8,128)S(1)}) custom-call(s32[1]{0:T(128)} %bitcast.side_ref, s32[1]{0:T(128)} %bitcast.1.place_ref, ...), custom_call_target="tpu_custom_call" | custom-call | tf_op jit(solution)/shard_map/pallas_call | solution.py:378
  95.3 4.5 %collective-permute-start.10 = (f32[40,80]{1,0:T(8,128)S(1)}, f32[40,80]{1,0:T(8,128)S(1)}, u32[]{:S(2)}, u32[]{:S(2)}) collective-permute-start(f32[40,80]{1,0:T(8,128)S(1)} %get-tuple-element.49), channel_id=1, source_target_pairs={{0,64},{64,128},{128,192},{192,0},{1,65},{65,129},{129,193},{193,1... | collective-permute-start | bytes 38408 | tf_op jit(solution)/shard_map/ppermute | solution.py:487
  99.8 2.6 %collective-permute-start.11 = (f32[40,80]{1,0:T(8,128)S(1)}, f32[40,80]{1,0:T(8,128)S(1)}, u32[]{:S(2)}, u32[]{:S(2)}) collective-permute-start(f32[40,80]{1,0:T(8,128)S(1)} %get-tuple-element.50), channel_id=1, source_target_pairs={{0,128},{64,192},{128,0},{192,64},{1,129},{65,193},{129,1},{193,65... | collective-permute-start | bytes 38408 | tf_op jit(solution)/shard_map/ppermute | solution.py:487
  102.4 2.9 %collective-permute-start.12 = (f32[40,80]{1,0:T(8,128)S(1)}, f32[40,80]{1,0:T(8,128)S(1)}, u32[]{:S(2)}, u32[]{:S(2)}) collective-permute-start(f32[40,80]{1,0:T(8,128)S(1)} %get-tuple-element.51), channel_id=1, source_target_pairs={{0,192},{64,0},{128,64},{192,128},{1,193},{65,1},{129,65},{193,129... | collective-permute-start | bytes 38408 | tf_op jit(solution)/shard_map/ppermute | solution.py:487
  107.1 4.6 %collective-permute-start.14 = (f32[40,80]{1,0:T(8,128)S(1)}, f32[40,80]{1,0:T(8,128)S(1)}, u32[]{:S(2)}, u32[]{:S(2)}) collective-permute-start(f32[40,80]{1,0:T(8,128)S(1)} %add_add_fusion.1), channel_id=1, source_target_pairs={{0,4},{1,5},{2,6},{3,7},{4,0},{5,1},{6,2},{7,3},{8,12},{9,13},{10,... | collective-permute-start | bytes 38408 | tf_op jit(solution)/shard_map/ppermute | solution.py:447
  111.6 1.8 %collective-permute-done.14 = f32[40,80]{1,0:T(8,128)S(1)} collective-permute-done((f32[40,80]{1,0:T(8,128)S(1)}, f32[40,80]{1,0:T(8,128)S(1)}, u32[]{:S(2)}, u32[]{:S(2)}) %collective-permute-start.14) | collective-permute-done | bytes 12832 | tf_op jit(solution)/shard_map/ppermute | solution.py:447
  113.7 5.6 %collective-permute-done.15 = f32[40,80]{1,0:T(8,128)S(1)} collective-permute-done((f32[40,80]{1,0:T(8,128)S(1)}, f32[40,80]{1,0:T(8,128)S(1)}, u32[]{:S(2)}, u32[]{:S(2)}) %collective-permute-start.15) | collective-permute-done | bytes 12832 | tf_op jit(solution)/shard_map/ppermute | solution.py:447
  120.1 3.0 %collective-permute-done.16 = f32[40,80]{1,0:T(8,128)S(1)} collective-permute-done((f32[40,80]{1,0:T(8,128)S(1)}, f32[40,80]{1,0:T(8,128)S(1)}, u32[]{:S(2)}, u32[]{:S(2)}) %collective-permute-start.16) | collective-permute-done | bytes 12832 | tf_op jit(solution)/shard_map/ppermute | solution.py:447
  123.3 4.8 %collective-permute-done.17 = f32[40,80]{1,0:T(8,128)S(1)} collective-permute-done((f32[40,80]{1,0:T(8,128)S(1)}, f32[40,80]{1,0:T(8,128)S(1)}, u32[]{:S(2)}, u32[]{:S(2)}) %collective-permute-start.17) | collective-permute-done | bytes 12832 | tf_op jit(solution)/shard_map/ppermute | solution.py:447
  128.4 3.2 %collective-permute-start.20 = (f32[40,80]{1,0:T(8,128)S(1)}, f32[40,80]{1,0:T(8,128)S(1)}, u32[]{:S(2)}, u32[]{:S(2)}) collective-permute-start(f32[40,80]{1,0:T(8,128)S(1)} %add.41), channel_id=1, source_target_pairs={{0,3},{1,2},{2,1},{3,0},{4,7},{5,6},{6,5},{7,4},{8,11},{9,10},{10,... | collective-permute-start | bytes 38408 | tf_op jit(solution)/shard_map/ppermute | solution.py:447
  (44 shorter events, 12.4 us)
Async XLA Ops:
  0.6 4.7 %copy-start = (f32[16,8,1024]{2,1,0:T(8,128)S(1)}, f32[16,8,1024]{2,1,0:T(8,128)}, u32[]{:S(2)}) copy-start(f32[16,8,1024]{2,1,0:T(8,128)} %refs_3_.1) | copy-start | bytes 1572868
  2.3 4.6 %collective-permute-start = (f32[25,8,128]{2,1,0:T(8,128)}, f32[25,8,128]{2,1,0:T(8,128)S(1)}, u32[]{:S(2)}, u32[]{:S(2)}) collective-permute-start(f32[25,8,128]{2,1,0:T(8,128)} %get-tuple-element.30), channel_id=1, source_target_pairs={{0,64},{64,128},{128,192},{1,65},{65,129},{129,193},{2,66},{66,130... | collective-permute-start | bytes 307208 | tf_op jit(solution)/shard_map/ppermute | solution.py:456
  4.1 6.2 %collective-permute-start.1 = (f32[25,8,128]{2,1,0:T(8,128)}, f32[25,8,128]{2,1,0:T(8,128)S(1)}, u32[]{:S(2)}, u32[]{:S(2)}) collective-permute-start(f32[25,8,128]{2,1,0:T(8,128)} %get-tuple-element.31), channel_id=1, source_target_pairs={{64,0},{128,64},{192,128},{65,1},{129,65},{193,129},{66,2},{130,66... | collective-permute-start | bytes 307208 | tf_op jit(solution)/shard_map/ppermute | solution.py:457
  10.3 54.9 %copy-start.4 = (f32[16]{0:T(128)S(1)}, f32[16]{0:T(128)}, u32[]{:S(2)}) copy-start(f32[16]{0:T(128)} %stiff_ref.1) | copy-start | bytes 196
  10.3 54.9 %copy-start.5 = (f32[16]{0:T(128)S(1)}, f32[16]{0:T(128)}, u32[]{:S(2)}) copy-start(f32[16]{0:T(128)} %dens_ref.1) | copy-start | bytes 196
  11.8 7.1 %collective-permute-start.2 = (f32[16,8,640]{2,1,0:T(8,128)S(1)}, f32[16,8,640]{2,1,0:T(8,128)S(1)}, u32[]{:S(2)}, u32[]{:S(2)}) collective-permute-start(f32[16,8,640]{2,1,0:T(8,128)S(1)} %get-tuple-element.33), channel_id=1, source_target_pairs={{0,1},{1,0},{2,3},{3,2},{4,5},{5,4},{6,7},{7,6},{8,9},{9,8},{10,11... | collective-permute-start | bytes 983048 | tf_op jit(solution)/shard_map/ppermute | solution.py:447
  18.9 58.3 %collective-permute-start.3 = (f32[32,8,640]{2,1,0:T(8,128)S(1)}, f32[32,8,640]{2,1,0:T(8,128)S(1)}, u32[]{:S(2)}, u32[]{:S(2)}) collective-permute-start(f32[32,8,640]{2,1,0:T(8,128)S(1)} %shard_map.80), channel_id=1, source_target_pairs={{0,2},{1,3},{2,4},{3,5},{4,6},{5,7},{6,8},{7,9},{8,10},{9,11},{10,... | collective-permute-start | bytes 1966088 | tf_op jit(solution)/shard_map/ppermute | solution.py:432
  22.7 54.4 %collective-permute-start.4 = (f32[32,8,640]{2,1,0:T(8,128)S(1)}, f32[32,8,640]{2,1,0:T(8,128)S(1)}, u32[]{:S(2)}, u32[]{:S(2)}) collective-permute-start(f32[32,8,640]{2,1,0:T(8,128)S(1)} %shard_map.80), channel_id=1, source_target_pairs={{2,0},{3,1},{4,2},{5,3},{6,4},{7,5},{8,6},{9,7},{10,8},{11,9},{12,... | collective-permute-start | bytes 1966088 | tf_op jit(solution)/shard_map/ppermute | solution.py:432
  28.8 5.6 %collective-permute-start.7 = (f32[9,8,640]{2,1,0:T(8,128)S(1)}, f32[9,8,640]{2,1,0:T(8,128)S(1)}, u32[]{:S(2)}, u32[]{:S(2)}) collective-permute-start(f32[9,8,640]{2,1,0:T(8,128)S(1)} %get-tuple-element.37), channel_id=1, source_target_pairs={{0,1},{1,0},{2,3},{3,2},{4,5},{5,4},{6,7},{7,6},{8,9},{9,8},{10,11... | collective-permute-start | bytes 552968 | tf_op jit(solution)/shard_map/ppermute | solution.py:447
  29.4 17.5 %collective-permute-start.5 = (f32[10,8,640]{2,1,0:T(8,128)S(1)}, f32[10,8,640]{2,1,0:T(8,128)S(1)}, u32[]{:S(2)}, u32[]{:S(2)}) collective-permute-start(f32[10,8,640]{2,1,0:T(8,128)S(1)} %get-tuple-element.34), channel_id=1, source_target_pairs={{1,5},{3,7},{4,0},{5,9},{6,2},{7,11},{8,4},{9,13},{10,6},{11,15},{... | collective-permute-start | bytes 614408 | tf_op jit(solution)/shard_map/ppermute | solution.py:438
  35.1 30.0 %collective-permute-start.8 = (f32[18,8,640]{2,1,0:T(8,128)}, f32[18,8,640]{2,1,0:T(8,128)}, u32[]{:S(2)}, u32[]{:S(2)}) collective-permute-start(f32[18,8,640]{2,1,0:T(8,128)} %shard_map.81), channel_id=1, source_target_pairs={{0,2},{1,3},{2,4},{3,5},{4,6},{5,7},{6,8},{7,9},{8,10},{9,11},{10,... | collective-permute-start | bytes 1105928 | tf_op jit(solution)/shard_map/ppermute | solution.py:432
  37.5 27.6 %collective-permute-start.9 = (f32[18,8,640]{2,1,0:T(8,128)}, f32[18,8,640]{2,1,0:T(8,128)}, u32[]{:S(2)}, u32[]{:S(2)}) collective-permute-start(f32[18,8,640]{2,1,0:T(8,128)} %shard_map.81), channel_id=1, source_target_pairs={{2,0},{3,1},{4,2},{5,3},{6,4},{7,5},{8,6},{9,7},{10,8},{11,9},{12,... | collective-permute-start | bytes 1105928 | tf_op jit(solution)/shard_map/ppermute | solution.py:432
  47.0 18.1 %collective-permute-start.6 = (f32[10,8,640]{2,1,0:T(8,128)}, f32[10,8,640]{2,1,0:T(8,128)S(1)}, u32[]{:S(2)}, u32[]{:S(2)}) collective-permute-start(f32[10,8,640]{2,1,0:T(8,128)} %get-tuple-element.35), channel_id=1, source_target_pairs={{1,4},{3,6},{4,1},{5,8},{6,3},{7,10},{8,5},{9,12},{10,7},{11,14},{... | collective-permute-start | bytes 614408 | tf_op jit(solution)/shard_map/ppermute | solution.py:438
  95.3 10.0 %collective-permute-start.10 = (f32[40,80]{1,0:T(8,128)S(1)}, f32[40,80]{1,0:T(8,128)S(1)}, u32[]{:S(2)}, u32[]{:S(2)}) collective-permute-start(f32[40,80]{1,0:T(8,128)S(1)} %get-tuple-element.49), channel_id=1, source_target_pairs={{0,64},{64,128},{128,192},{192,0},{1,65},{65,129},{129,193},{193,1... | collective-permute-start | bytes 38408 | tf_op jit(solution)/shard_map/ppermute | solution.py:487
  99.8 5.5 %collective-permute-start.11 = (f32[40,80]{1,0:T(8,128)S(1)}, f32[40,80]{1,0:T(8,128)S(1)}, u32[]{:S(2)}, u32[]{:S(2)}) collective-permute-start(f32[40,80]{1,0:T(8,128)S(1)} %get-tuple-element.50), channel_id=1, source_target_pairs={{0,128},{64,192},{128,0},{192,64},{1,129},{65,193},{129,1},{193,65... | collective-permute-start | bytes 38408 | tf_op jit(solution)/shard_map/ppermute | solution.py:487
  102.4 4.4 %collective-permute-start.12 = (f32[40,80]{1,0:T(8,128)S(1)}, f32[40,80]{1,0:T(8,128)S(1)}, u32[]{:S(2)}, u32[]{:S(2)}) collective-permute-start(f32[40,80]{1,0:T(8,128)S(1)} %get-tuple-element.51), channel_id=1, source_target_pairs={{0,192},{64,0},{128,64},{192,128},{1,193},{65,1},{129,65},{193,129... | collective-permute-start | bytes 38408 | tf_op jit(solution)/shard_map/ppermute | solution.py:487
  106.8 27.4 %collective-permute-start.13 = (f32[24,8,512]{2,1,0:T(8,128)S(1)}, f32[24,8,512]{2,1,0:T(8,128)S(1)}, u32[]{:S(2)}, u32[]{:S(2)}) collective-permute-start(f32[24,8,512]{2,1,0:T(8,128)S(1)} %get-tuple-element.52), channel_id=1, source_target_pairs={{0,1},{1,0},{2,3},{3,2},{4,5},{5,4},{6,7},{7,6},{8,9},{9,8},{10,11... | collective-permute-start | bytes 1179656 | tf_op jit(solution)/shard_map/ppermute | solution.py:447
  107.1 6.3 %collective-permute-start.14 = (f32[40,80]{1,0:T(8,128)S(1)}, f32[40,80]{1,0:T(8,128)S(1)}, u32[]{:S(2)}, u32[]{:S(2)}) collective-permute-start(f32[40,80]{1,0:T(8,128)S(1)} %add_add_fusion.1), channel_id=1, source_target_pairs={{0,4},{1,5},{2,6},{3,7},{4,0},{5,1},{6,2},{7,3},{8,12},{9,13},{10,... | collective-permute-start | bytes 38408 | tf_op jit(solution)/shard_map/ppermute | solution.py:447
  113.4 5.9 %collective-permute-start.15 = (f32[40,80]{1,0:T(8,128)S(1)}, f32[40,80]{1,0:T(8,128)S(1)}, u32[]{:S(2)}, u32[]{:S(2)}) collective-permute-start(f32[40,80]{1,0:T(8,128)S(1)} %add.38), channel_id=1, source_target_pairs={{0,12},{1,13},{2,14},{3,15},{4,8},{5,9},{6,10},{7,11},{8,4},{9,5},... | collective-permute-start | bytes 38408 | tf_op jit(solution)/shard_map/ppermute | solution.py:447
  119.3 3.8 %collective-permute-start.16 = (f32[40,80]{1,0:T(8,128)S(1)}, f32[40,80]{1,0:T(8,128)S(1)}, u32[]{:S(2)}, u32[]{:S(2)}) collective-permute-start(f32[40,80]{1,0:T(8,128)S(1)} %add.39), channel_id=1, source_target_pairs={{0,16},{1,17},{2,18},{3,19},{4,20},{5,21},{6,22},{7,23},{8,24},{9,... | collective-permute-start | bytes 38408 | tf_op jit(solution)/shard_map/ppermute | solution.py:447
  123.1 5.0 %collective-permute-start.17 = (f32[40,80]{1,0:T(8,128)S(1)}, f32[40,80]{1,0:T(8,128)S(1)}, u32[]{:S(2)}, u32[]{:S(2)}) collective-permute-start(f32[40,80]{1,0:T(8,128)S(1)} %add.40), channel_id=1, source_target_pairs={{0,48},{1,49},{2,50},{3,51},{4,52},{5,53},{6,54},{7,55},{8,56},{9,... | collective-permute-start | bytes 38408 | tf_op jit(solution)/shard_map/ppermute | solution.py:447
  128.1 3.8 %collective-permute-start.18 = (f32[40,80]{1,0:T(8,128)S(1)}, f32[40,80]{1,0:T(8,128)S(1)}, u32[]{:S(2)}, u32[]{:S(2)}) collective-permute-start(f32[40,80]{1,0:T(8,128)S(1)} %add.41), channel_id=1, source_target_pairs={{0,1},{1,0},{2,3},{3,2},{4,5},{5,4},{6,7},{7,6},{8,9},{9,8},{10,11... | collective-permute-start | bytes 38408 | tf_op jit(solution)/shard_map/ppermute | solution.py:447
  128.4 3.8 %collective-permute-start.19 = (f32[40,80]{1,0:T(8,128)S(1)}, f32[40,80]{1,0:T(8,128)S(1)}, u32[]{:S(2)}, u32[]{:S(2)}) collective-permute-start(f32[40,80]{1,0:T(8,128)S(1)} %add.41), channel_id=1, source_target_pairs={{0,2},{1,3},{2,0},{3,1},{4,6},{5,7},{6,4},{7,5},{8,10},{9,11},{10,... | collective-permute-start | bytes 38408 | tf_op jit(solution)/shard_map/ppermute | solution.py:447
  128.4 5.2 %collective-permute-start.20 = (f32[40,80]{1,0:T(8,128)S(1)}, f32[40,80]{1,0:T(8,128)S(1)}, u32[]{:S(2)}, u32[]{:S(2)}) collective-permute-start(f32[40,80]{1,0:T(8,128)S(1)} %add.41), channel_id=1, source_target_pairs={{0,3},{1,2},{2,1},{3,0},{4,7},{5,6},{6,5},{7,4},{8,11},{9,10},{10,... | collective-permute-start | bytes 38408 | tf_op jit(solution)/shard_map/ppermute | solution.py:447
  (3 other events, 14.2 us)
